TPU v7x, 32 devices: a whole 2x2x4 slice. The times are simulated.
32 devices in a mesh: grp: 2 (over x), lat: 16 (over z, y, core).
Axes of the slice: x: 2, y: 2, z: 4, core: 2. Of those that a mesh axis runs over, the one named last changes fastest.
Arguments:
- coarse: bfloat16 [80, 64, 512], P(None, ('grp', 'lat')), parts along dimension 1, may hold values from -6 to 6
- reg_gain: float32 [2, 80], replicated, may hold values from 0.25 to 1.75
- reg_weight: bfloat16 [2, 3, 3, 80, 80], replicated, may hold values from -0.21875 to 0.21875
- reg_bias: float32 [2, 80], replicated, may hold values from -1.5 to 1.5
- noisy: bfloat16 [32, 4, 32, 512], P(('grp', 'lat')), parts along dimension 0, may hold values from -6 to 6
- lift_weight: bfloat16 [3, 3, 192, 84], replicated, may hold values from -0.21875 to 0.21875
- lift_bias: float32 [192], replicated, may hold values from -1.5 to 1.5
- mid_gain: float32 [192], replicated, may hold values from 0.25 to 1.75
- mid_weight: bfloat16 [3, 3, 192, 192], replicated, may hold values from -0.15625 to 0.15625
- mid_bias: float32 [192], replicated, may hold values from -1.5 to 1.5
Outputs:
- fine_level: bfloat16 [32, 192, 32, 512], P(('grp', 'lat')), parts along dimension 0
There are 2 independent parts, one for each index of `grp`. A program takes and returns all parts, laid end to end along the dimension named above; an argument that names none is the same for every part. Nothing has to cross between parts.
All inputs are finite; a program needn't handle non-finite values.
Results may differ from a plain program's by a relative error of at most 0.007.
Values may be sent and summed in bfloat16 or wider, within the bound.
A program may use at most 320 MiB of HBM per device.

v0:
```python
import jax
import jax.numpy as jnp
from jax import lax
from jax.sharding import PartitionSpec as P

TILE_COLS = 4
LAT_UP = 4
LON_UP = 4


EPSILON = 1e-06


def from_partner(shard, axis, distance):
    return lax.ppermute(shard, axis, [(i, i ^ 1 << distance) for i in range(lax.axis_size(axis))])


def passed_along(block, axis, distance):
    devices = range(lax.axis_size(axis))
    route = [(i - distance, i) for i in devices if i - distance in devices]
    return lax.ppermute(block, axis, route)


def extended(shard, sides, width):
    for axis, dim in sides:
        size, length = (lax.axis_size(axis), shard.shape[dim])
        up = [(i, (i + 1) % size) for i in range(size - 1)]
        down = [(j, i) for i, j in up]
        last = lax.slice_in_dim(shard, length - width, length, axis=dim)
        initial = lax.slice_in_dim(shard, 0, width, axis=dim)
        before = lax.ppermute(last, axis, up)
        after = lax.ppermute(initial, axis, down)
        shard = jnp.concatenate([before, shard, after], axis=dim)
    return shard


def activate(field_in, gain_row):
    values = field_in.astype(jnp.float32)
    inverse = lax.rsqrt(jnp.mean(values * values, axis=0, keepdims=True) + EPSILON)
    return jax.nn.silu(values * inverse * gain_row[:, None, None]).astype(jnp.bfloat16)


def wrap_cols(field_in):
    return jnp.concatenate([field_in[:, :, -1:], field_in, field_in[:, :, :1]], axis=2)


def conv_taps(padded, weight):
    height = padded.shape[1] - 2
    breadth = padded.shape[2] - 2
    summed = jnp.zeros((weight.shape[2], height, breadth), jnp.float32)
    for row_shift in range(3):
        for col_shift in range(3):
            window = padded[:, row_shift : row_shift + height, col_shift : col_shift + breadth]
            summed = summed + jnp.einsum(
                "oc,crl->orl",
                weight[row_shift, col_shift],
                window,
                preferred_element_type=jnp.float32,
            )
    return summed


def spread(values, axis, factor):
    count = values.shape[axis]
    pieces = []
    for phase in range(factor):
        numerator = 2 * phase + 1 - factor
        offset = numerator // (2 * factor)
        weight = (numerator - 2 * factor * offset) / (2.0 * factor)
        lower = lax.slice_in_dim(values, 1 + offset, count - 1 + offset, axis=axis)
        upper = lax.slice_in_dim(values, 2 + offset, count + offset, axis=axis)
        pieces.append((1.0 - weight) * lower + weight * upper)
    stacked = jnp.stack(pieces, axis=axis + 1)
    shape = list(values.shape)
    shape[axis] = (count - 2) * factor
    return stacked.reshape(shape)


def tile_halo(field_in, rim_width, device):
    tile_col = device % TILE_COLS
    east_edge = field_in[:, :, -rim_width:]
    west_edge = field_in[:, :, :rim_width]
    even_col = tile_col % 2 == 0
    paired = from_partner(jnp.where(even_col, east_edge, west_edge), "lat", 0)
    relayed = from_partner(jnp.where(even_col, west_edge, east_edge), "lat", 1)
    crossed = from_partner(relayed, "lat", 0)
    west_cells = jnp.where(even_col, crossed, paired)
    east_cells = jnp.where(even_col, paired, crossed)
    widened = jnp.concatenate([west_cells, field_in, east_cells], axis=2)
    north_cells = passed_along(widened[:, -rim_width:], "lat", TILE_COLS)
    south_cells = passed_along(widened[:, :rim_width], "lat", -TILE_COLS)
    return jnp.concatenate([north_cells, widened, south_cells], axis=1)


def upsample(halo_tile, rim_width, fine_rim, tile_row, ct_rows, ct_lon, coarse_total):
    rows = halo_tile.shape[1]
    global_row = tile_row * ct_rows - rim_width + jnp.arange(rows, dtype=jnp.int32)
    values = halo_tile.astype(jnp.float32)
    top_row = values[:, rim_width : rim_width + 1]
    bottom_row = values[:, rows - rim_width - 1 : rows - rim_width]
    values = jnp.where((global_row < 0)[None, :, None], top_row, values)
    values = jnp.where((global_row >= coarse_total)[None, :, None], bottom_row, values)
    halfway = spread(values, 1, LAT_UP)
    row_start = LAT_UP * (rim_width - 1) - fine_rim
    halfway = lax.slice_in_dim(
        halfway, row_start, row_start + LAT_UP * ct_rows + 2 * fine_rim, axis=1
    )
    fine_field = spread(halfway, 2, LON_UP)
    col_start = LON_UP * (rim_width - 1) - fine_rim
    return lax.slice_in_dim(
        fine_field, col_start, col_start + LON_UP * ct_lon + 2 * fine_rim, axis=2
    )


def per_device(
    coarse,
    reg_gain,
    reg_weight,
    reg_bias,
    noisy,
    lift_weight,
    lift_bias,
    mid_gain,
    mid_weight,
    mid_bias,
):
    device = lax.axis_index("lat")
    devices_lat = lax.axis_size("lat")
    channels = coarse.shape[0]
    band_rows = coarse.shape[1]
    coarse_total = band_rows * devices_lat
    blocks = reg_weight.shape[0]
    current = coarse
    for block_index in range(blocks):
        activated = activate(current, reg_gain[block_index])
        padded = extended(activated, (("lat", 1),), 1)
        update = conv_taps(wrap_cols(padded), reg_weight[block_index])
        updated = current.astype(jnp.float32) + update + reg_bias[block_index][:, None, None]
        current = lax.optimization_barrier(updated.astype(jnp.bfloat16))
    tile_col = device % TILE_COLS
    tile_row = device // TILE_COLS
    ct_lon = coarse.shape[2] // TILE_COLS
    ct_rows = band_rows * TILE_COLS
    pieces = current.reshape(channels, band_rows, TILE_COLS, ct_lon)
    assembled = jnp.zeros((channels, ct_rows, ct_lon), jnp.bfloat16)
    for partner_mask in range(TILE_COLS):
        partner_col = jnp.bitwise_xor(tile_col, partner_mask)
        block_data = lax.dynamic_index_in_dim(pieces, partner_col, 2, keepdims=False)
        if partner_mask & 2:
            block_data = from_partner(block_data, "lat", 1)
        if partner_mask & 1:
            block_data = from_partner(block_data, "lat", 0)
        row_start = partner_col * band_rows
        assembled = lax.dynamic_update_slice(
            assembled, block_data, (jnp.int32(0), row_start, jnp.int32(0))
        )
    fine_rows = noisy.shape[2]
    fine_total = fine_rows * devices_lat // TILE_COLS
    noise_tile = noisy[0]
    halo_tile = tile_halo(assembled, 2, device)
    fine_field = upsample(halo_tile, 2, 2, tile_row, ct_rows, ct_lon, coarse_total)
    row_index = tile_row * fine_rows - 2 + jnp.arange(fine_rows + 4, dtype=jnp.int32)
    inside = (row_index >= 0) & (row_index < fine_total)
    fine_field = jnp.where(inside[None, :, None], fine_field, 0.0).astype(jnp.bfloat16)
    noise_halo = tile_halo(noise_tile, 2, device)
    lift_input = jnp.concatenate([fine_field, noise_halo], axis=0)
    lifted = conv_taps(lift_input, lift_weight) + lift_bias[:, None, None]
    lifted = lax.optimization_barrier(lifted.astype(jnp.bfloat16))
    activated = activate(lifted, mid_gain)
    inner_rows = inside[1:-1]
    activated = jnp.where(inner_rows[None, :, None], activated, jnp.zeros_like(activated))
    summed = (
        lifted[:, 1:-1, 1:-1].astype(jnp.float32)
        + conv_taps(activated, mid_weight)
        + mid_bias[:, None, None]
    )
    return summed.astype(jnp.bfloat16)[None]


def solution(mesh):
    placed = (
        P(None, ("grp", "lat"), None),
        P(),
        P(),
        P(),
        P(("grp", "lat"), None, None, None),
        P(),
        P(),
        P(),
        P(),
        P(),
    )
    return jax.shard_map(
        per_device,
        mesh=mesh,
        in_specs=placed,
        out_specs=P(("grp", "lat"), None, None, None),
        check_vma=False,
    )
```

profile of v0, /device:TPU:0, one launch (start us, length us, event | category | flops | bytes accessed | tf_op | source)
XLA Modules:
  0.0 306.3 jit_solution(12104860826136978543)
XLA Ops:
  0.0 1.0 copy.64
  1.2 3.1 collective-permute-start.13
  6.0 1.1 fusion.71
  7.1 2.4 collective-permute-start
  9.5 1.3 collective-permute-start.1
  15.1 4.5 %collective-permute-start.2 = (bf16[80,1,512]{2,0,1:T(8,128)(2,1)S(1)}, bf16[80,1,512]{2,0,1:T(8,128)(2,1)S(1)}, u32[]{:S(2)}, u32[]{:S(2)}) collective-permute-start(bf16[80,1,512]{2,0,1:T(8,128)(2,1)S(1)} %get-tuple-element.31), channel_id=1, source_target_pairs={{0,1},{1,2},{2,3},{3,4},{4,5},{5,6},{6,7},{7,8},{8,9},{9,10},{10,1... | collective-permute-start | bytes 245768 | tf_op jit(solution)/shard_map/ppermute | solution.py:31
  19.7 1.3 collective-permute-start.3
  21.0 1.2 collective-permute-start.14
  25.5 4.6 %collective-permute-start.4 = (bf16[80,2,128]{2,0,1:T(8,128)(2,1)S(1)}, bf16[80,2,128]{2,0,1:T(8,128)(2,1)S(1)}, u32[]{:S(2)}, u32[]{:S(2)}) collective-permute-start(bf16[80,2,128]{2,0,1:T(8,128)(2,1)S(1)} %bitcast.307), channel_id=1, source_target_pairs={{0,1},{1,0},{2,3},{3,2},{4,5},{5,4},{6,7},{7,6},{8,9},{9,8},{10,11... | collective-permute-start | bytes 122888 | tf_op jit(solution)/shard_map/ppermute | solution.py:15
  30.0 2.5 collective-permute-start.5
  33.0 1.6 collective-permute-done.5
  34.7 1.9 collective-permute-done.6
  36.6 1.2 collective-permute-done.7
  38.6 3.1 %collective-permute-done.8 = bf16[80,8,2]{0,2,1:T(2,128)(2,1)S(1)} collective-permute-done((bf16[80,8,2]{0,2,1:T(2,128)(2,1)S(1)}, bf16[80,8,2]{0,2,1:T(2,128)(2,1)S(1)}, u32[]{:S(2)}, u32[]{:S(2)}) %collective-permute-start.8) | collective-permute-done | bytes 2592 | tf_op jit(solution)/shard_map/ppermute | solution.py:15
  41.7 1.1 collective-permute-done.9
  42.9 3.5 %collective-permute-start.11 = (bf16[80,2,132]{0,2,1:T(8,128)(2,1)S(1)}, bf16[80,2,132]{0,2,1:T(8,128)(2,1)S(1)}, u32[]{:S(2)}, u32[]{:S(2)}) collective-permute-start(bf16[80,2,132]{0,2,1:T(8,128)(2,1)S(1)} %get-tuple-element.21), channel_id=1, source_target_pairs={{0,4},{1,5},{2,6},{3,7},{4,8},{5,9},{6,10},{7,11},{8,12},{9,13},{1... | collective-permute-start | bytes 126728 | tf_op jit(solution)/shard_map/ppermute | solution.py:21
  46.4 1.3 collective-permute-start.12
  47.8 4.5 %collective-permute-start.16 = (bf16[4,2,516]{2,0,1:T(4,128)(2,1)S(1)}, bf16[4,2,516]{2,0,1:T(4,128)(2,1)S(1)}, u32[]{:S(2)}, u32[]{:S(2)}) collective-permute-start(bf16[4,2,516]{2,0,1:T(4,128)(2,1)S(1)} %get-tuple-element.25), channel_id=1, source_target_pairs={{0,4},{1,5},{2,6},{3,7},{4,8},{5,9},{6,10},{7,11},{8,12},{9,13},{1... | collective-permute-start | bytes 24776 | tf_op jit(solution)/shard_map/ppermute | solution.py:21
  52.3 1.5 collective-permute-start.17
  54.6 1.6 add_bitcast_fusion.3
  56.3 1.3 pad_maximum_fusion
  57.6 1.8 copy.47
  59.4 3.9 %slice.486 = bf16[80,36,516]{0,2,1:T(8,128)(2,1)} slice(bf16[80,36,520]{0,2,1:T(8,128)(2,1)S(1)} %bitcast.291), slice={[0:80], [0:36], [2:518]} | slice | bytes 5944320 | tf_op jit(solution)/shard_map/slice | solution.py:110
  63.3 6.6 %copy.55 = bf16[80,36,516]{2,0,1:T(8,128)(2,1)} copy(bf16[80,36,516]{0,2,1:T(8,128)(2,1)} %slice.486) | data formatting | bytes 5944320
  69.9 3.0 select_convert_fusion
  72.9 4.1 %maximum_maximum_fusion = bf16[84,36,516]{2,0,1:T(8,128)(2,1)S(1)} fusion(bf16[4,2,516]{2,0,1:T(4,128)(2,1)S(1)} %collective-permute-done.17, bf16[4,32,2]{2,0,1:T(4,128)(2,1)S(1)} %bitcast.298, bf16[4,32,512]{2,0,1:T(4,128)(2,1)S(1)} %bitcast.294, bf16[4,32,2]{2,0,1:T(4,128)(2,1)S(1)} %bitcast.296, bf16[4,2,516]{2,0,1:T(4,128)(2,1)S(1)} %collective-permute-done.16, ...), kind=kLoop, calls=%fused_computation.37 | loop fusion | flops 18724608 | bytes 6241536 | tf_op jit(solution)/shard_map/concatenate | solution.py:166
  77.0 4.0 %fusion.158 = bf16[84,34,514]{2,0,1:T(8,128)(2,1)} fusion(bf16[84,36,516]{2,0,1:T(8,128)(2,1)S(1)} %maximum_maximum_fusion), kind=kLoop, calls=%fused_computation.38.clone.2 | loop fusion | bytes 5871936 | tf_op jit(solution)/shard_map/oc,crl->orl/dot_general | solution.py:54
  81.0 8.2 %fusion.34 = f32[34,514,192]{1,2,0:T(8,128)} fusion(bf16[84,36,516]{2,0,1:T(8,128)(2,1)S(1)} %maximum_maximum_fusion, bf16[3,3,192,84]{2,3,1,0:T(8,128)(2,1)S(1)} %copy-done.4), kind=kOutput, calls=%fused_computation.39 | convolution fusion | flops 563705856 | bytes 17296384 | tf_op jit(solution)/shard_map/oc,crl->orl/dot_general | solution.py:54
  89.2 8.1 %fusion.36 = f32[34,514,192]{1,2,0:T(8,128)} fusion(bf16[84,36,516]{2,0,1:T(8,128)(2,1)S(1)} %maximum_maximum_fusion, bf16[3,3,192,84]{2,3,1,0:T(8,128)(2,1)S(1)} %copy-done.4), kind=kOutput, calls=%fused_computation.41 | convolution fusion | flops 563705856 | bytes 17296384 | tf_op jit(solution)/shard_map/oc,crl->orl/dot_general | solution.py:54
  97.3 8.2 %fusion.38 = f32[34,514,192]{1,2,0:T(8,128)} fusion(bf16[84,36,516]{2,0,1:T(8,128)(2,1)S(1)} %maximum_maximum_fusion, bf16[3,3,192,84]{2,3,1,0:T(8,128)(2,1)S(1)} %copy-done.4), kind=kOutput, calls=%fused_computation.43 | convolution fusion | flops 563705856 | bytes 17296384 | tf_op jit(solution)/shard_map/oc,crl->orl/dot_general | solution.py:54
  105.5 8.2 %fusion.40 = f32[34,514,192]{1,2,0:T(8,128)} fusion(bf16[84,36,516]{2,0,1:T(8,128)(2,1)S(1)} %maximum_maximum_fusion, bf16[3,3,192,84]{2,3,1,0:T(8,128)(2,1)S(1)} %copy-done.4), kind=kOutput, calls=%fused_computation.45 | convolution fusion | flops 563705856 | bytes 17296384 | tf_op jit(solution)/shard_map/oc,crl->orl/dot_general | solution.py:54
  113.7 8.4 %fusion.42 = f32[34,514,192]{1,2,0:T(8,128)} fusion(bf16[84,36,516]{2,0,1:T(8,128)(2,1)S(1)} %maximum_maximum_fusion, bf16[3,3,192,84]{2,3,1,0:T(8,128)(2,1)S(1)} %copy-done.4), kind=kOutput, calls=%fused_computation.47 | convolution fusion | flops 563705856 | bytes 17296384 | tf_op jit(solution)/shard_map/oc,crl->orl/dot_general | solution.py:54
  122.0 8.3 %fusion.44 = f32[34,514,192]{1,2,0:T(8,128)} fusion(bf16[84,36,516]{2,0,1:T(8,128)(2,1)S(1)} %maximum_maximum_fusion, bf16[3,3,192,84]{2,3,1,0:T(8,128)(2,1)S(1)} %copy-done.4), kind=kOutput, calls=%fused_computation.49 | convolution fusion | flops 563705856 | bytes 17296384 | tf_op jit(solution)/shard_map/oc,crl->orl/dot_general | solution.py:54
  130.3 8.2 %fusion.46 = f32[34,514,192]{1,2,0:T(8,128)} fusion(bf16[84,36,516]{2,0,1:T(8,128)(2,1)S(1)} %maximum_maximum_fusion, bf16[3,3,192,84]{2,3,1,0:T(8,128)(2,1)S(1)} %copy-done.4), kind=kOutput, calls=%fused_computation.51 | convolution fusion | flops 563705856 | bytes 17296384 | tf_op jit(solution)/shard_map/oc,crl->orl/dot_general | solution.py:54
  138.5 8.1 %fusion.48 = f32[34,514,192]{1,2,0:T(8,128)} fusion(bf16[84,36,516]{2,0,1:T(8,128)(2,1)S(1)} %maximum_maximum_fusion, bf16[3,3,192,84]{2,3,1,0:T(8,128)(2,1)S(1)} %copy-done.4), kind=kOutput, calls=%fused_computation.53 | convolution fusion | flops 563705856 | bytes 17296384 | tf_op jit(solution)/shard_map/oc,crl->orl/dot_general | solution.py:54
  146.5 46.7 %fusion.30 = bf16[192,34,514]{2,0,1:T(8,128)(2,1)} fusion(f32[192]{0:T(256)S(1)} %copy-done.7, f32[34,514,192]{1,2,0:T(8,128)} %fusion.34, f32[34,514,192]{1,2,0:T(8,128)} %fusion.36, f32[34,514,192]{1,2,0:T(8,128)} %fusion.38, f32[34,514,192]{1,2,0:T(8,128)} %fusion.40, f32[34,514,192]{1,2,0:T(8,128)} %fusion.42, f32[34,514,192]{1,2,0:T(8,128)} %fusion.44, ...), kind=kOutput, calls=%fused_computation.36 | convolution fusion | flops 597259776 | bytes 117065376 | tf_op jit(solution)/shard_map/oc,crl->orl/dot_general | solution.py:54
  193.2 5.4 %fusion = f32[34,514]{1,0:T(8,128)S(1)} fusion(bf16[192,34,514]{2,0,1:T(8,128)(2,1)} %fusion.30), kind=kLoop, calls=%fused_computation.2 | loop fusion | flops 10048700 | bytes 6780688 | tf_op jit(solution)/shard_map/reduce_sum | solution.py:39
  199.0 6.1 %fusion.10 = bf16[192,34,514]{2,0,1:T(8,128)(2,1)S(1)} fusion(bf16[192,34,514]{2,0,1:T(8,128)(2,1)S(1)} %copy-done.1, f32[192]{0:T(256)S(1)} %copy-done.6, f32[34,514]{1,0:T(8,128)S(1)} %add_rsqrt_fusion, pred[34]{0:T(512)(128)(4,1)S(1)} %slice.423), kind=kLoop, calls=%fused_computation.15 | loop fusion | flops 30198528 | bytes 13492274 | tf_op jit(solution)/shard_map/jit(_where)/select_n | solution.py:171
  205.1 7.0 %fusion.11 = f32[32,512,192]{1,2,0:T(8,128)} fusion(bf16[192,34,514]{2,0,1:T(8,128)(2,1)S(1)} %fusion.10, bf16[3,3,192,192]{3,2,1,0:T(8,128)(2,1)S(1)} %copy-done.3), kind=kOutput, calls=%fused_computation.17 | convolution fusion | flops 1207959552 | bytes 18972672 | tf_op jit(solution)/shard_map/oc,crl->orl/dot_general | solution.py:54
  212.1 6.7 %fusion.13 = f32[32,512,192]{1,2,0:T(8,128)} fusion(bf16[192,34,514]{2,0,1:T(8,128)(2,1)S(1)} %fusion.10, bf16[3,3,192,192]{3,2,1,0:T(8,128)(2,1)S(1)} %copy-done.3), kind=kOutput, calls=%fused_computation.19 | convolution fusion | flops 1207959552 | bytes 18972672 | tf_op jit(solution)/shard_map/oc,crl->orl/dot_general | solution.py:54
  218.8 6.4 %fusion.15 = f32[32,512,192]{1,2,0:T(8,128)} fusion(bf16[192,34,514]{2,0,1:T(8,128)(2,1)S(1)} %fusion.10, bf16[3,3,192,192]{3,2,1,0:T(8,128)(2,1)S(1)} %copy-done.3), kind=kOutput, calls=%fused_computation.21 | convolution fusion | flops 1207959552 | bytes 18972672 | tf_op jit(solution)/shard_map/oc,crl->orl/dot_general | solution.py:54
  225.1 6.6 %fusion.17 = f32[32,512,192]{1,2,0:T(8,128)} fusion(bf16[192,34,514]{2,0,1:T(8,128)(2,1)S(1)} %fusion.10, bf16[3,3,192,192]{3,2,1,0:T(8,128)(2,1)S(1)} %copy-done.3), kind=kOutput, calls=%fused_computation.23 | convolution fusion | flops 1207959552 | bytes 18972672 | tf_op jit(solution)/shard_map/oc,crl->orl/dot_general | solution.py:54
  231.8 6.6 %fusion.19 = f32[32,512,192]{1,2,0:T(8,128)} fusion(bf16[192,34,514]{2,0,1:T(8,128)(2,1)S(1)} %fusion.10, bf16[3,3,192,192]{3,2,1,0:T(8,128)(2,1)S(1)} %copy-done.3), kind=kOutput, calls=%fused_computation.25 | convolution fusion | flops 1207959552 | bytes 18972672 | tf_op jit(solution)/shard_map/oc,crl->orl/dot_general | solution.py:54
  238.4 6.3 %fusion.21 = f32[32,512,192]{1,2,0:T(8,128)} fusion(bf16[192,34,514]{2,0,1:T(8,128)(2,1)S(1)} %fusion.10, bf16[3,3,192,192]{3,2,1,0:T(8,128)(2,1)S(1)} %copy-done.3), kind=kOutput, calls=%fused_computation.27 | convolution fusion | flops 1207959552 | bytes 18972672 | tf_op jit(solution)/shard_map/oc,crl->orl/dot_general | solution.py:54
  244.7 6.9 %fusion.23 = f32[32,512,192]{1,2,0:T(8,128)} fusion(bf16[192,34,514]{2,0,1:T(8,128)(2,1)S(1)} %fusion.10, bf16[3,3,192,192]{3,2,1,0:T(8,128)(2,1)S(1)} %copy-done.3), kind=kOutput, calls=%fused_computation.29 | convolution fusion | flops 1207959552 | bytes 18972672 | tf_op jit(solution)/shard_map/oc,crl->orl/dot_general | solution.py:54
  251.6 6.7 %fusion.25 = f32[32,512,192]{1,2,0:T(8,128)} fusion(bf16[192,34,514]{2,0,1:T(8,128)(2,1)S(1)} %fusion.10, bf16[3,3,192,192]{3,2,1,0:T(8,128)(2,1)S(1)} %copy-done.3), kind=kOutput, calls=%fused_computation.31 | convolution fusion | flops 1207959552 | bytes 18972672 | tf_op jit(solution)/shard_map/oc,crl->orl/dot_general | solution.py:54
  258.3 38.6 %fusion.29 = bf16[1,192,32,512]{3,1,2,0:T(8,128)(2,1)} fusion(f32[192]{0:T(256)S(1)} %copy-done.5, f32[32,512,192]{1,2,0:T(8,128)} %fusion.11, f32[32,512,192]{1,2,0:T(8,128)} %fusion.13, f32[32,512,192]{1,2,0:T(8,128)} %fusion.15, f32[32,512,192]{1,2,0:T(8,128)} %fusion.17, f32[32,512,192]{1,2,0:T(8,128)} %fusion.19, f32[32,512,192]{1,2,0:T(8,128)} %fusion.21, ...), kind=kOutput, calls=%fused_computation.35 | convolution fusion | flops 1245708288 | bytes 119636992 | tf_op jit(solution)/shard_map/oc,crl->orl/dot_general | solution.py:54
  296.9 9.0 %copy.50 = bf16[1,192,32,512]{3,2,1,0:T(8,128)(2,1)} copy(bf16[1,192,32,512]{3,1,2,0:T(8,128)(2,1)} %fusion.29) | data formatting | bytes 12582912 | tf_op jit(solution)/shard_map/broadcast_in_dim | solution.py:177
  (94 shorter events, 11.8 us)
Async XLA Ops:
  0.0 14.7 %copy-start.2 = (bf16[80,2,512]{2,1,0:T(2,128)(2,1)S(1)}, bf16[80,2,512]{2,1,0:T(2,128)(2,1)}, u32[]{:S(2)}) copy-start(bf16[80,2,512]{2,1,0:T(2,128)(2,1)} %param.10) | copy-start | bytes 491524
  1.2 19.9 %collective-permute-start.13 = (bf16[4,32,2]{2,0,1:T(4,128)(2,1)S(1)}, bf16[4,32,2]{2,0,1:T(4,128)(2,1)S(1)}, u32[]{:S(2)}, u32[]{:S(2)}) collective-permute-start(bf16[4,32,2]{2,0,1:T(4,128)(2,1)S(1)} %get-tuple-element.35), channel_id=1, source_target_pairs={{0,2},{1,3},{2,0},{3,1},{4,6},{5,7},{6,4},{7,5},{8,10},{9,11},{10,... | collective-permute-start | bytes 1544 | tf_op jit(solution)/shard_map/ppermute | solution.py:15
  4.2 37.4 %collective-permute-start.15 = (bf16[4,32,2]{2,0,1:T(4,128)(2,1)S(1)}, bf16[4,32,2]{2,0,1:T(4,128)(2,1)S(1)}, u32[]{:S(2)}, u32[]{:S(2)}) collective-permute-start(bf16[4,32,2]{2,0,1:T(4,128)(2,1)S(1)} %get-tuple-element.36), channel_id=1, source_target_pairs={{0,1},{1,0},{2,3},{3,2},{4,5},{5,4},{6,7},{7,6},{8,9},{9,8},{10,11... | collective-permute-start | bytes 1544 | tf_op jit(solution)/shard_map/ppermute | solution.py:15
  7.1 5.5 %collective-permute-start = (bf16[80,1,512]{2,0,1:T(8,128)(2,1)S(1)}, bf16[80,1,512]{2,0,1:T(8,128)(2,1)S(1)}, u32[]{:S(2)}, u32[]{:S(2)}) collective-permute-start(bf16[80,1,512]{2,0,1:T(8,128)(2,1)S(1)} %get-tuple-element.33), channel_id=1, source_target_pairs={{0,1},{1,2},{2,3},{3,4},{4,5},{5,6},{6,7},{7,8},{8,9},{9,10},{10,1... | collective-permute-start | bytes 245768 | tf_op jit(solution)/shard_map/ppermute | solution.py:31
  9.5 3.2 %collective-permute-start.1 = (bf16[80,1,512]{2,0,1:T(8,128)(2,1)S(1)}, bf16[80,1,512]{2,0,1:T(8,128)(2,1)S(1)}, u32[]{:S(2)}, u32[]{:S(2)}) collective-permute-start(bf16[80,1,512]{2,0,1:T(8,128)(2,1)S(1)} %get-tuple-element.34), channel_id=1, source_target_pairs={{1,0},{2,1},{3,2},{4,3},{5,4},{6,5},{7,6},{8,7},{9,8},{10,9},{11,1... | collective-permute-start | bytes 245768 | tf_op jit(solution)/shard_map/ppermute | solution.py:32
  15.1 7.1 %collective-permute-start.2 = (bf16[80,1,512]{2,0,1:T(8,128)(2,1)S(1)}, bf16[80,1,512]{2,0,1:T(8,128)(2,1)S(1)}, u32[]{:S(2)}, u32[]{:S(2)}) collective-permute-start(bf16[80,1,512]{2,0,1:T(8,128)(2,1)S(1)} %get-tuple-element.31), channel_id=1, source_target_pairs={{0,1},{1,2},{2,3},{3,4},{4,5},{5,6},{6,7},{7,8},{8,9},{9,10},{10,1... | collective-permute-start | bytes 245768 | tf_op jit(solution)/shard_map/ppermute | solution.py:31
  19.7 3.2 %collective-permute-start.3 = (bf16[80,1,512]{2,0,1:T(8,128)(2,1)S(1)}, bf16[80,1,512]{2,0,1:T(8,128)(2,1)S(1)}, u32[]{:S(2)}, u32[]{:S(2)}) collective-permute-start(bf16[80,1,512]{2,0,1:T(8,128)(2,1)S(1)} %get-tuple-element.32), channel_id=1, source_target_pairs={{1,0},{2,1},{3,2},{4,3},{5,4},{6,5},{7,6},{8,7},{9,8},{10,9},{11,1... | collective-permute-start | bytes 245768 | tf_op jit(solution)/shard_map/ppermute | solution.py:32
  21.0 20.6 %collective-permute-start.14 = (bf16[4,32,2]{2,0,1:T(4,128)(2,1)S(1)}, bf16[4,32,2]{2,0,1:T(4,128)(2,1)S(1)}, u32[]{:S(2)}, u32[]{:S(2)}) collective-permute-start(bf16[4,32,2]{2,0,1:T(4,128)(2,1)S(1)} %collective-permute-done.13), channel_id=1, source_target_pairs={{0,1},{1,0},{2,3},{3,2},{4,5},{5,4},{6,7},{7,6},{8,9},{9,8},{10,11... | collective-permute-start | bytes 1544 | tf_op jit(solution)/shard_map/ppermute | solution.py:15
  25.5 7.3 %collective-permute-start.4 = (bf16[80,2,128]{2,0,1:T(8,128)(2,1)S(1)}, bf16[80,2,128]{2,0,1:T(8,128)(2,1)S(1)}, u32[]{:S(2)}, u32[]{:S(2)}) collective-permute-start(bf16[80,2,128]{2,0,1:T(8,128)(2,1)S(1)} %bitcast.307), channel_id=1, source_target_pairs={{0,1},{1,0},{2,3},{3,2},{4,5},{5,4},{6,7},{7,6},{8,9},{9,8},{10,11... | collective-permute-start | bytes 122888 | tf_op jit(solution)/shard_map/ppermute | solution.py:15
  30.0 4.5 %collective-permute-start.5 = (bf16[80,2,128]{2,0,1:T(8,128)(2,1)S(1)}, bf16[80,2,128]{2,0,1:T(8,128)(2,1)S(1)}, u32[]{:S(2)}, u32[]{:S(2)}) collective-permute-start(bf16[80,2,128]{2,0,1:T(8,128)(2,1)S(1)} %bitcast.306), channel_id=1, source_target_pairs={{0,2},{1,3},{2,0},{3,1},{4,6},{5,7},{6,4},{7,5},{8,10},{9,11},{10,... | collective-permute-start | bytes 122888 | tf_op jit(solution)/shard_map/ppermute | solution.py:15
  32.6 4.0 %collective-permute-start.6 = (bf16[80,2,128]{2,0,1:T(8,128)(2,1)S(1)}, bf16[80,2,128]{2,0,1:T(8,128)(2,1)S(1)}, u32[]{:S(2)}, u32[]{:S(2)}) collective-permute-start(bf16[80,2,128]{2,0,1:T(8,128)(2,1)S(1)} %bitcast.305), channel_id=1, source_target_pairs={{0,2},{1,3},{2,0},{3,1},{4,6},{5,7},{6,4},{7,5},{8,10},{9,11},{10,... | collective-permute-start | bytes 122888 | tf_op jit(solution)/shard_map/ppermute | solution.py:15
  36.6 1.2 collective-permute-start.7
  38.0 3.7 %collective-permute-start.8 = (bf16[80,8,2]{0,2,1:T(2,128)(2,1)S(1)}, bf16[80,8,2]{0,2,1:T(2,128)(2,1)S(1)}, u32[]{:S(2)}, u32[]{:S(2)}) collective-permute-start(bf16[80,8,2]{0,2,1:T(2,128)(2,1)S(1)} %get-tuple-element.23), channel_id=1, source_target_pairs={{0,2},{1,3},{2,0},{3,1},{4,6},{5,7},{6,4},{7,5},{8,10},{9,11},{10,... | collective-permute-start | bytes 7688 | tf_op jit(solution)/shard_map/ppermute | solution.py:15
  38.6 3.1 %collective-permute-start.10 = (bf16[80,8,2]{0,2,1:T(2,128)(2,1)S(1)}, bf16[80,8,2]{0,2,1:T(2,128)(2,1)S(1)}, u32[]{:S(2)}, u32[]{:S(2)}) collective-permute-start(bf16[80,8,2]{0,2,1:T(2,128)(2,1)S(1)} %get-tuple-element.24), channel_id=1, source_target_pairs={{0,1},{1,0},{2,3},{3,2},{4,5},{5,4},{6,7},{7,6},{8,9},{9,8},{10,11... | collective-permute-start | bytes 7688 | tf_op jit(solution)/shard_map/ppermute | solution.py:15
  41.6 1.2 collective-permute-start.9
  42.9 11.0 %collective-permute-start.11 = (bf16[80,2,132]{0,2,1:T(8,128)(2,1)S(1)}, bf16[80,2,132]{0,2,1:T(8,128)(2,1)S(1)}, u32[]{:S(2)}, u32[]{:S(2)}) collective-permute-start(bf16[80,2,132]{0,2,1:T(8,128)(2,1)S(1)} %get-tuple-element.21), channel_id=1, source_target_pairs={{0,4},{1,5},{2,6},{3,7},{4,8},{5,9},{6,10},{7,11},{8,12},{9,13},{1... | collective-permute-start | bytes 126728 | tf_op jit(solution)/shard_map/ppermute | solution.py:21
  46.4 7.5 %collective-permute-start.12 = (bf16[80,2,132]{0,2,1:T(8,128)(2,1)S(1)}, bf16[80,2,132]{0,2,1:T(8,128)(2,1)S(1)}, u32[]{:S(2)}, u32[]{:S(2)}) collective-permute-start(bf16[80,2,132]{0,2,1:T(8,128)(2,1)S(1)} %get-tuple-element.22), channel_id=1, source_target_pairs={{4,0},{5,1},{6,2},{7,3},{8,4},{9,5},{10,6},{11,7},{12,8},{13,9},{1... | collective-permute-start | bytes 126728 | tf_op jit(solution)/shard_map/ppermute | solution.py:21
  47.8 25.2 %collective-permute-start.16 = (bf16[4,2,516]{2,0,1:T(4,128)(2,1)S(1)}, bf16[4,2,516]{2,0,1:T(4,128)(2,1)S(1)}, u32[]{:S(2)}, u32[]{:S(2)}) collective-permute-start(bf16[4,2,516]{2,0,1:T(4,128)(2,1)S(1)} %get-tuple-element.25), channel_id=1, source_target_pairs={{0,4},{1,5},{2,6},{3,7},{4,8},{5,9},{6,10},{7,11},{8,12},{9,13},{1... | collective-permute-start | bytes 24776 | tf_op jit(solution)/shard_map/ppermute | solution.py:21
  52.3 20.6 %collective-permute-start.17 = (bf16[4,2,516]{2,0,1:T(4,128)(2,1)S(1)}, bf16[4,2,516]{2,0,1:T(4,128)(2,1)S(1)}, u32[]{:S(2)}, u32[]{:S(2)}) collective-permute-start(bf16[4,2,516]{2,0,1:T(4,128)(2,1)S(1)} %get-tuple-element.26), channel_id=1, source_target_pairs={{4,0},{5,1},{6,2},{7,3},{8,4},{9,5},{10,6},{11,7},{12,8},{13,9},{1... | collective-permute-start | bytes 24776 | tf_op jit(solution)/shard_map/ppermute | solution.py:21
  72.9 8.1 %copy-start.4 = (bf16[3,3,192,84]{2,3,1,0:T(8,128)(2,1)S(1)}, bf16[3,3,192,84]{2,3,1,0:T(8,128)(2,1)}, u32[]{:S(2)}) copy-start(bf16[3,3,192,84]{2,3,1,0:T(8,128)(2,1)} %param.15) | copy-start | bytes 870916
  138.5 8.1 %copy-start.7 = (f32[192]{0:T(256)S(1)}, f32[192]{0:T(256)}, u32[]{:S(2)}) copy-start(f32[192]{0:T(256)} %param.16) | copy-start | bytes 2308
  193.2 5.7 %copy-start.1 = (bf16[192,34,514]{2,0,1:T(8,128)(2,1)S(1)}, bf16[192,34,514]{2,0,1:T(8,128)(2,1)}, u32[]{:S(2)}) copy-start(bf16[192,34,514]{2,0,1:T(8,128)(2,1)} %fusion.30) | copy-start | bytes 20132356
  193.2 5.7 %copy-start.6 = (f32[192]{0:T(256)S(1)}, f32[192]{0:T(256)}, u32[]{:S(2)}) copy-start(f32[192]{0:T(256)} %param.17) | copy-start | bytes 2308
  199.0 6.1 %copy-start.3 = (bf16[3,3,192,192]{3,2,1,0:T(8,128)(2,1)S(1)}, bf16[3,3,192,192]{3,2,1,0:T(8,128)(2,1)}, u32[]{:S(2)}) copy-start(bf16[3,3,192,192]{3,2,1,0:T(8,128)(2,1)} %param.18) | copy-start | bytes 1990660
  205.1 46.5 %copy-start = (bf16[192,34,514]{2,0,1:T(8,128)(2,1)}, bf16[192,34,514]{2,0,1:T(8,128)(2,1)S(1)}, u32[]{:S(2)}) copy-start(bf16[192,34,514]{2,0,1:T(8,128)(2,1)S(1)} %fusion.10) | copy-start | bytes 20132356
  251.6 6.7 %copy-start.5 = (f32[192]{0:T(256)S(1)}, f32[192]{0:T(256)}, u32[]{:S(2)}) copy-start(f32[192]{0:T(256)} %param.19) | copy-start | bytes 2308
where the time goes:
time: 311 us; the launch traced here: 306 us
  matrix products  208 us (67%)
  starting transfers between devices  32.2 us (10%)
  local copies, waits for them, and re-layouts  30.4 us (10%)
  other arithmetic  25.5 us (8%)
  waiting for transfers between devices  9.6 us (3%)
    dot_general x36, matrix products, conv_taps(): jnp.einsum('oc,crl->orl', weight[row_shift, col_shift], window, preferred...  208 us
    ppermute x10, starting transfers between devices, from_partner(): lax.ppermute(shard, axis, [(i, i ^ 1 << distance) for i in range(lax.axis...  11.9 us
    ppermute x4, starting transfers between devices, passed_along(): return lax.ppermute(block, axis, route)  10.8 us
    broadcast_in_dim x1, local copies, waits for them, and re-layouts, per_device(): return summed.astype(jnp.bfloat16)[None]  9.02 us
    ppermute x10, waiting for transfers between devices, from_partner(): lax.ppermute(shard, axis, [(i, i ^ 1 << distance) for i in range(lax.axis...  8.91 us
    unnamed x21, local copies, waits for them, and re-layouts  7.98 us
    ppermute x2, starting transfers between devices, extended(): before = lax.ppermute(last, axis, up)  6.94 us
    reduce_sum x3, other arithmetic, activate(): jnp.mean(values * values, axis=0, keepdims=True) + EPSILON  6.42 us
  transfers between devices with their start and end apart: 18, of which 7 were waited for; matrix products, arithmetic and copies ran while one was open for 10% of the time, Pallas kernels for 0%

commit v1 on v0

v1 whole, which is shorter than its diff:
```python
import functools

import jax
import jax.numpy as jnp
from jax import lax
from jax.experimental import pallas as pl
from jax.experimental.pallas import tpu as pltpu
from jax.sharding import PartitionSpec as P

TILE_COLS = 4
LAT_UP = 4
LON_UP = 4
EPSILON = 1e-06
F32 = jnp.float32
BF16 = jnp.bfloat16
MESH = pl.DeviceIdType.MESH
HALF = 64


def gather_kernel(pieces, cols, rows, got, got_cols, got_rows, send, recv, nsend, nrecv, local):
    me = lax.axis_index("lat")
    tile_rows = lax.axis_size("lat") // TILE_COLS
    r = me // TILE_COLS
    c = me % TILE_COLS
    north, south = r > 0, r < tile_rows - 1

    barrier = pltpu.get_barrier_semaphore()

    def greet(target):
        pl.semaphore_signal(barrier, inc=1, device_id={"lat": target}, device_id_type=MESH)

    for k in range(1, TILE_COLS):
        greet(r * TILE_COLS + (c + k) % TILE_COLS)

    @pl.when(north)
    def _():
        for k in range(TILE_COLS):
            greet((r - 1) * TILE_COLS + k)

    @pl.when(south)
    def _():
        for k in range(TILE_COLS):
            greet((r + 1) * TILE_COLS + k)

    peers = TILE_COLS - 1 + jnp.where(north, TILE_COLS, 0) + jnp.where(south, TILE_COLS, 0)
    pl.semaphore_wait(barrier, peers)

    def remote(src, dst, ssem, rsem, target):
        return pltpu.make_async_remote_copy(
            src_ref=src, dst_ref=dst, send_sem=ssem, recv_sem=rsem,
            device_id={"lat": target}, device_id_type=MESH)

    def band_copy(k, row, slot, ssem):
        col = (c + k) % TILE_COLS
        return remote(pieces.at[col], got.at[slot], send.at[ssem], recv.at[slot], row * TILE_COLS + col)

    west, east = (c + TILE_COLS - 1) % TILE_COLS, (c + 1) % TILE_COLS

    def col_copy(slot, row, col):
        return remote(cols, got_cols.at[slot], nsend.at[slot], nrecv.at[slot], row * TILE_COLS + col)

    def row_copy(slot, row):
        return remote(rows, got_rows.at[slot], nsend.at[6 + slot], nrecv.at[6 + slot], row * TILE_COLS + c)

    low, high = c < 2, c >= 2

    def each(action):
        @pl.when(jnp.logical_and(south, high))
        def _():
            for k in range(TILE_COLS):
                action(band_copy(k, r + 1, c - 2, TILE_COLS + k))

        @pl.when(jnp.logical_and(north, low))
        def _():
            for k in range(TILE_COLS):
                action(band_copy(k, r - 1, 6 + c, TILE_COLS + k))

        for k in range(1, TILE_COLS):
            action(band_copy(k, r, 2 + c, k))
        action(col_copy(0, r, east))
        action(col_copy(1, r, west))

        @pl.when(south)
        def _():
            action(row_copy(0, r + 1))
            action(col_copy(2, r + 1, east))
            action(col_copy(3, r + 1, west))

        @pl.when(north)
        def _():
            action(row_copy(1, r - 1))
            action(col_copy(4, r - 1, east))
            action(col_copy(5, r - 1, west))

    each(lambda copy: copy.start())
    own = pltpu.make_async_copy(pieces.at[c], got.at[2 + c], local)
    own.start()
    own.wait()
    each(lambda copy: copy.wait_send())

    def arrived(slot):
        remote(pieces.at[0], got.at[slot], send.at[0], recv.at[slot], me).wait_recv()

    def edge(slot):
        if slot < 6:
            remote(cols, got_cols.at[slot], nsend.at[slot], nrecv.at[slot], me).wait_recv()
        else:
            remote(rows, got_rows.at[slot - 6], nsend.at[slot], nrecv.at[slot], me).wait_recv()

    for k in range(1, TILE_COLS):
        arrived(2 + (c + k) % TILE_COLS)
    edge(0)
    edge(1)

    @pl.when(north)
    def _():
        arrived(0)
        arrived(1)
        edge(2)
        edge(3)
        edge(6)

    @pl.when(south)
    def _():
        arrived(6)
        arrived(7)
        edge(4)
        edge(5)
        edge(7)


def gather(pieces, cols, rows):
    any_space = pl.BlockSpec(memory_space=pl.ANY)
    dma = pltpu.SemaphoreType.DMA
    return pl.pallas_call(
        gather_kernel,
        out_shape=(
            jax.ShapeDtypeStruct((8,) + pieces.shape[1:], BF16),
            jax.ShapeDtypeStruct((6,) + cols.shape, BF16),
            jax.ShapeDtypeStruct((2,) + rows.shape, BF16),
        ),
        in_specs=[any_space] * 3,
        out_specs=(any_space,) * 3,
        scratch_shapes=[dma((2 * TILE_COLS,)), dma((8,)), dma((8,)), dma((8,)), dma],
        compiler_params=pltpu.CompilerParams(collective_id=0, has_side_effects=True),
    )(pieces, cols, rows)


def silu(values):
    return 0.5 * values * (1.0 + jnp.tanh(0.5 * values))


def activate(values, gain):
    inverse = lax.rsqrt(jnp.mean(values * values, axis=0, keepdims=True) + EPSILON)
    return silu(values * inverse * gain)


def split(numerator, factor):
    lower = numerator // (2 * factor)
    return lower, (numerator - 2 * factor * lower).astype(F32) / (2.0 * factor)


def tile_kernel(
    dims, info, got, gain, regw, regb, noise, noise_edge, liftw, liftb, midg, midw, midb, out,
    taps, field, lon, lines, upper, sides, bands, keep, rows_out, stage, sems,
):
    cin, ch, ct, fr, fl = dims
    bands_n = got.shape[0]
    cw = got.shape[2]
    ccols = fl // LON_UP
    tile_row, tile_rows = info[0], info[1]
    top, bottom = tile_row == 0, tile_row == tile_rows - 1
    spare = (bands_n - ct) // 2

    def real(i):
        row = tile_row * ct - spare + i
        return jnp.logical_and(row >= 0, row < ct * tile_rows)

    blocks = regw.shape[0]
    for k in range(blocks):
        first, last = 1 + k, bands_n - 1 - k

        def fill(i, _, k=k):
            source = got[i] if k == 0 else field[i]
            values = jnp.where(real(i), source.astype(F32), 0.0)
            values = jnp.where(real(i), activate(values, gain[k]), 0.0)
            base = pl.multiple_of(i * 3 * cin, 16)
            taps[pl.ds(base, cin), :] = pltpu.roll(values, 1, 1).astype(BF16)
            taps[pl.ds(base + cin, cin), :] = values.astype(BF16)
            taps[pl.ds(base + 2 * cin, cin), :] = pltpu.roll(values, cw - 1, 1).astype(BF16)
            return 0

        lax.fori_loop(first, last, fill, 0)

        def conv(i, _, k=k):
            base = pl.multiple_of((i - 1) * 3 * cin, 16)
            update = jnp.dot(regw[k], taps[pl.ds(base, 9 * cin), :], preferred_element_type=F32)
            source = got[i] if k == 0 else field[i]
            field[i] = jnp.where(real(i), source.astype(F32) + update + regb[k], 0.0).astype(BF16)
            return 0

        lax.fori_loop(first + 1, last - 1, conv, 0)

    first = 1 + blocks
    count = bands_n - 2 * first
    coarse_lane = lax.broadcasted_iota(jnp.int32, (cw, 3 * fl), 0)
    position = lax.broadcasted_iota(jnp.int32, (cw, 3 * fl), 1)

    def lon_weights(fine_col, lane):
        lower, part = split(2 * fine_col + 1 - LON_UP, LON_UP)
        low_lane = jnp.where(lower < 0, lower + cw, lower)
        high_lane = jnp.where(lower + 1 < 0, lower + 1 + cw, lower + 1)
        return (jnp.where(lane == low_lane, 1.0 - part, 0.0)
                + jnp.where(lane == high_lane, part, 0.0)).astype(BF16)

    shift = jnp.where(position >= 2 * fl, 2, jnp.where(position >= fl, 1, 0))
    lon[...] = lon_weights(position - shift * fl + shift - 1, coarse_lane)
    edge_lane = lax.broadcasted_iota(jnp.int32, (cw, 128), 0)
    edge_pos = lax.broadcasted_iota(jnp.int32, (cw, 128), 1)
    edge_col = jnp.where(edge_pos < 3, edge_pos - 2, fl - 4 + edge_pos)
    edge_weights = lon_weights(edge_col, edge_lane)

    def widen(i, _):
        for q in range(3):
            lines[i, q * cin:(q + 1) * cin, :] = jnp.dot(
                field[i + first], lon[:, q * fl:(q + 1) * fl], preferred_element_type=F32)
        return 0

    lax.fori_loop(0, count, widen, 0)

    low_line = jnp.where(top, 1, 0)
    high_line = jnp.where(bottom, count - 2, count - 1)
    fine_total = fr * tile_rows

    def inside(t):
        row = tile_row * fr + t - 2
        return jnp.logical_and(row >= 0, row < fine_total)

    slab = 3 * cin + noise.shape[1]

    def raise_row(t):
        lower, part = split(2 * (t - 2) + 1 - LAT_UP + 2 * LAT_UP, LAT_UP)
        a = jnp.clip(lower, low_line, high_line)
        b = jnp.clip(lower + 1, low_line, high_line)
        blended = (1.0 - part) * lines[a] + part * lines[b]
        base = pl.multiple_of(t * slab, 16)
        upper[pl.ds(base, 3 * cin), :] = jnp.where(inside(t), blended, 0.0).astype(BF16)
        upper[pl.ds(base + 3 * cin, noise.shape[1]), :] = noise[t]

    lane = lax.broadcasted_iota(jnp.int32, (1, 128), 1)
    left = lane < HALF
    edge_row = jnp.where(left, lane, lane - HALF)
    sums = [[jnp.zeros((cin, 128), F32) for _ in range(3)] for _ in range(3)]
    weights = []
    for p in range(3):
        t = edge_row + p
        lower, part = split(2 * (t - 2) + 1 - LAT_UP + 2 * LAT_UP, LAT_UP)
        a = jnp.clip(lower, low_line, high_line)
        b = jnp.clip(lower + 1, low_line, high_line)
        ok = inside(t)
        weights.append([jnp.where(ok, jnp.where(a == i, 1.0 - part, 0.0) + jnp.where(b == i, part, 0.0), 0.0)
                        for i in range(count)])
    for i in range(count):
        narrow = jnp.dot(field[first + i], edge_weights, preferred_element_type=F32)
        for q in range(3):
            column = jnp.where(left, narrow[:, q:q + 1], narrow[:, 3 + q:4 + q])
            for p in range(3):
                sums[p][q] = sums[p][q] + weights[p][i] * column
    for p in range(3):
        for q in range(3):
            base = p * slab + q * cin
            sides[base:base + cin, :] = sums[p][q].astype(BF16)
        sides[p * slab + 3 * cin:(p + 1) * slab, :] = noise_edge[p]
    edge_lift = jnp.dot(liftw[...], sides[...], preferred_element_type=F32) + liftb[...]
    edge_lift = edge_lift.astype(BF16).astype(F32)
    edge_act = jnp.where(inside(edge_row + 1), activate(edge_lift, midg[...]), 0.0)

    for t in range(3):
        raise_row(jnp.int32(t))

    lane_full = lax.broadcasted_iota(jnp.int32, (1, fl), 1)
    kept = keep.shape[0]
    group = stage.shape[2]

    def lift(l):
        base = pl.multiple_of(l * slab, 16)
        return jnp.dot(liftw[...], upper[pl.ds(base, 3 * slab), :], preferred_element_type=F32) + liftb[...]

    def finish(l, lifted):
        rounded = lifted.astype(BF16)
        keep[l % kept] = rounded
        values = jnp.where(inside(l + 1), activate(rounded.astype(F32), midg[...]), 0.0)
        turned = pltpu.roll(edge_act, 128 - l, 1)
        edge_l = jnp.concatenate([turned[:, :128]] + [turned] * (fl // 128 - 1), axis=1)
        turned_r = pltpu.roll(edge_act, HALF - 1 - l + 128, 1)
        edge_r = jnp.concatenate([turned_r] * (fl // 128), axis=1)
        base = pl.multiple_of(l * 3 * ch, 16)
        bands[pl.ds(base, ch), :] = jnp.where(lane_full == 0, edge_l, pltpu.roll(values, 1, 1)).astype(BF16)
        bands[pl.ds(base + ch, ch), :] = values.astype(BF16)
        bands[pl.ds(base + 2 * ch, ch), :] = jnp.where(
            lane_full == fl - 1, edge_r, pltpu.roll(values, fl - 1, 1)).astype(BF16)

    def mid(y):
        base = pl.multiple_of(y * 3 * ch, 16)
        return jnp.dot(midw[...], bands[pl.ds(base, 9 * ch), :], preferred_element_type=F32)

    def flush(y):
        part = y // group
        slot = part % 2

        def copy(n):
            return pltpu.make_async_copy(
                stage.at[n % 2], out.at[0, :, pl.ds(pl.multiple_of(n * group, group), group), :], sems.at[n % 2])

        @pl.when(part >= 2)
        def _():
            copy(part - 2).wait()

        def shrink(o, _):
            for j in range(fl // 128):
                block = rows_out[j, pl.ds(pl.multiple_of(o * 8 * group, 8 * group), 8 * group), :]
                stage[slot, pl.ds(o * 8, 8), :, j * 128:(j + 1) * 128] = block.reshape(8, group, 128).astype(BF16)
            return 0

        lax.fori_loop(0, ch // 8, shrink, 0)
        copy(part).start()

    def emit(y, product):
        total = keep[(y + 1) % kept].astype(F32) + product + midb[...]
        for j in range(fl // 128):
            rows_out[j, pl.ds(y % group, ch, stride=group), :] = total[:, j * 128:(j + 1) * 128]

        @pl.when(y % group == group - 1)
        def _():
            flush(y)

    def lead(l, _):
        lifted = lift(l)
        raise_row(l + 3)
        finish(l, lifted)
        return 0

    lax.fori_loop(0, 3, lead, 0)

    def both(l, _):
        lifted = lift(l)
        product = mid(l - 3)
        raise_row(jnp.minimum(l + 3, fr + 3))
        finish(l, lifted)
        emit(l - 3, product)
        return 0

    lax.fori_loop(3, fr + 2, both, 0)
    emit(fr - 1, mid(fr - 1))
    parts = fr // group
    for n in range(max(parts - 2, 0), parts):
        pltpu.make_async_copy(stage.at[n % 2], out.at[0, :, pl.ds(n * group, group), :], sems.at[n % 2]).wait()


def tile_program(info, got, gain, regw, regb, noise, noise_edge, liftw, liftb, midg, midw, midb, ct):
    cin, cw = got.shape[1], got.shape[2]
    ch = liftw.shape[0]
    fr, fl = noise.shape[0] - 4, noise.shape[2]
    count = ct + 2
    group = 16
    vmem = pl.BlockSpec(memory_space=pltpu.VMEM)
    slab = 3 * cin + noise.shape[1]
    return pl.pallas_call(
        functools.partial(tile_kernel, (cin, ch, ct, fr, fl)),
        out_shape=jax.ShapeDtypeStruct((1, ch, fr, fl), BF16),
        in_specs=[pl.BlockSpec(memory_space=pltpu.SMEM)] + [vmem] * 11,
        out_specs=pl.BlockSpec(memory_space=pl.ANY),
        scratch_shapes=[
            pltpu.VMEM((got.shape[0] * 3 * cin, cw), BF16),
            pltpu.VMEM(got.shape, BF16),
            pltpu.VMEM((cw, 3 * fl), BF16),
            pltpu.VMEM((count, 3 * cin, fl), F32),
            pltpu.VMEM(((fr + 4) * slab, fl), BF16),
            pltpu.VMEM((3 * slab, 128), BF16),
            pltpu.VMEM(((fr + 2) * 3 * ch, fl), BF16),
            pltpu.VMEM((8, ch, fl), BF16),
            pltpu.VMEM((fl // 128, ch * group, 128), F32),
            pltpu.VMEM((2, ch, group, fl), BF16),
            pltpu.SemaphoreType.DMA((2,)),
        ],
        compiler_params=pltpu.CompilerParams(vmem_limit_bytes=66_000_000),
    )(info, got, gain, regw, regb, noise, noise_edge, liftw, liftb, midg, midw, midb)


def per_device(
    coarse, reg_gain, reg_weight, reg_bias, noisy, lift_weight, lift_bias, mid_gain, mid_weight, mid_bias,
):
    device = lax.axis_index("lat")
    tile_rows = lax.axis_size("lat") // TILE_COLS
    cin, band_rows, clon = coarse.shape
    ct = band_rows * TILE_COLS
    ct_lon = clon // TILE_COLS
    blocks = reg_weight.shape[0]
    ch = lift_weight.shape[2]
    nout = noisy.shape[1]
    fr, fl = noisy.shape[2], noisy.shape[3]

    wide = coarse.reshape(cin, band_rows, TILE_COLS, ct_lon)
    after = jnp.roll(wide, -1, axis=2)
    before = jnp.roll(wide, 1, axis=2)
    side = jnp.where(jnp.arange(ct_lon) < ct_lon // 2, after, before)
    pieces = jnp.concatenate([wide, side], axis=3).transpose(2, 1, 0, 3)

    tile = noisy[0]
    edge_cols = jnp.concatenate([tile[:, :, :2], tile[:, :, -2:]], axis=2).transpose(0, 2, 1)
    edge_cols = jnp.pad(edge_cols.reshape(nout * 4, fr), ((0, 0), (0, 128 - fr)))
    edge_rows = jnp.concatenate([tile[:, :2], tile[:, -2:]], axis=1).reshape(nout * 4, fl)

    got, got_cols, got_rows = gather(pieces, edge_cols, edge_rows)

    tile_row = device // TILE_COLS
    has_north = tile_row > 0
    has_south = tile_row < tile_rows - 1
    nc = got_cols[:, :, :fr].reshape(6, nout, 4, fr).transpose(0, 1, 3, 2)
    nr = got_rows.reshape(2, nout, 4, fl)
    zero = jnp.zeros((), BF16)
    north = jnp.where(has_north, jnp.concatenate([nc[2][:, -2:, 2:], nr[0][:, 2:], nc[3][:, -2:, :2]], axis=2), zero)
    south = jnp.where(has_south, jnp.concatenate([nc[4][:, :2, 2:], nr[1][:, :2], nc[5][:, :2, :2]], axis=2), zero)
    middle = jnp.concatenate([nc[0][:, :, 2:], tile, nc[1][:, :, :2]], axis=2)
    whole = jnp.concatenate([north, middle, south], axis=1).transpose(1, 0, 2)
    spare = (-3 * nout) % 16
    noise = jnp.concatenate(
        [whole[:, :, 1 + q:1 + q + fl] for q in range(3)] + [jnp.zeros((fr + 4, spare, fl), BF16)], axis=1)
    sides = []
    for p in range(3):
        per_shift = []
        for q in range(3):
            lo = jnp.pad(whole[p:p + fr + 2, :, q].T, ((0, 0), (0, HALF - fr - 2)))
            hi = jnp.pad(whole[p:p + fr + 2, :, fl + 1 + q].T, ((0, 0), (0, HALF - fr - 2)))
            per_shift.append(jnp.concatenate([lo, hi], axis=1))
        sides.append(jnp.concatenate(per_shift + [jnp.zeros((spare, 128), BF16)], axis=0))
    noise_edge = jnp.stack(sides)

    regw = reg_weight.transpose(0, 3, 1, 2, 4).reshape(blocks, cin, 9 * cin)
    up = lift_weight[..., :cin].transpose(2, 0, 1, 3).reshape(ch, 3, 3 * cin)
    down = lift_weight[..., cin:].transpose(2, 0, 1, 3).reshape(ch, 3, 3 * nout)
    liftw = jnp.concatenate([up, down, jnp.zeros((ch, 3, spare), BF16)], axis=2).reshape(ch, -1)
    midw = mid_weight.transpose(2, 0, 1, 3).reshape(ch, 9 * ch)
    info = jnp.stack([tile_row, jnp.int32(tile_rows)]).astype(jnp.int32)
    got = got.reshape((got.shape[0] * band_rows,) + got.shape[2:])
    return tile_program(
        info, got, reg_gain[:, :, None], regw, reg_bias[:, :, None], noise, noise_edge,
        liftw, lift_bias[:, None], mid_gain[:, None], midw, mid_bias[:, None], ct)


def solution(mesh):
    placed = (
        P(None, ("grp", "lat"), None),
        P(),
        P(),
        P(),
        P(("grp", "lat"), None, None, None),
        P(),
        P(),
        P(),
        P(),
        P(),
    )
    return jax.shard_map(
        per_device,
        mesh=mesh,
        in_specs=placed,
        out_specs=P(("grp", "lat"), None, None, None),
        check_vma=False,
    )
```

time: 311 us -> 91.5 us (0.29); the launches traced: 306 us -> 91.1 us
  matrix products: 208 us -> 0 us
  Pallas kernels: 0 us -> 65 us
  starting transfers between devices: 32.2 us -> 0 us
  other arithmetic: 25.5 us -> 4.99 us
  local copies, waits for them, and re-layouts: 30.4 us -> 20.7 us
  waiting for transfers between devices: 9.6 us -> 0 us
    dot_general x36 -> x0, matrix products: 208 us -> none  [conv_taps(): jnp.einsum('oc,crl->orl', weight[row_shift, col_shift], window, preferred...]
    pallas_call x0 -> x2, Pallas kernels: none -> 65 us  [the longest x1 50.4 us: tile_program(): pl.pallas_call(functools.partial(tile_kernel, (cin, ch, ct, fr, fl)), out...]
    ppermute x18 -> x0, starting transfers between devices: 32.2 us -> none  [the longest x10 11.9 us: from_partner(): lax.ppermute(shard, axis, [(i, i ^ 1 << distance) for i in range(lax.axis...]
    ppermute x18 -> x0, waiting for transfers between devices: 9.6 us -> none  [the longest x10 8.91 us: from_partner(): lax.ppermute(shard, axis, [(i, i ^ 1 << distance) for i in range(lax.axis...]
    unnamed x21 -> x8, local copies, waits for them, and re-layouts: 7.98 us -> 1.09 us
    reduce_sum x3 -> x0, other arithmetic: 6.42 us -> none  [activate(): jnp.mean(values * values, axis=0, keepdims=True) + EPSILON]
    select_n x6 -> x3, other arithmetic: 6.47 us -> 0.2 us  [the longest x1 0.08 us: per_device(): jnp.where(has_south, jnp.concatenate([nc[4][:, :2, 2:], nr[1][:, :2], nc[...]
    reshape x1 -> x9, local copies, waits for them, and re-layouts: 0.04 us -> 4.9 us  [the longest x1 1.15 us: per_device(): midw = mid_weight.transpose(2, 0, 1, 3).reshape(ch, 9 * ch)]
  transfers between devices with their start and end apart: 18 -> 0, of which waited for: 7 -> 0; matrix products, arithmetic and copies ran while one was open for 10% -> 0% of each run, Pallas kernels for 0% -> 0%
where the time goes in v1:
time: 91.5 us; the launch traced here: 91.1 us
  Pallas kernels  65 us (71%)
  local copies, waits for them, and re-layouts  20.7 us (23%)
  other arithmetic  4.99 us (5%)
    pallas_call x1, Pallas kernels, tile_program(): pl.pallas_call(functools.partial(tile_kernel, (cin, ch, ct, fr, fl)), out...  50.4 us
    pallas_call x1, Pallas kernels, gather(): pl.pallas_call(gather_kernel, out_shape=(jax.ShapeDtypeStruct((8,) + piec...  14.6 us

profile of v1, /device:TPU:0, one launch (start us, length us, event | category | flops | bytes accessed | tf_op | source)
XLA Modules:
  0.0 91.1 jit_solution(13230734083132144736)
XLA Ops:
  0.0 0.6 pad_add_fusion.info
  0.6 0.1 pad.108.clone
  0.7 0.1 pad.80.clone
  0.8 0.8 slice_bitcast_fusion
  1.6 1.4 %copy.174.gain = f32[2,80,1]{2,1,0:T(8,128)} copy(f32[2,80,1]{1,0,2:T(2,128)} %bitcast.140) | data formatting | bytes 1280 | tf_op jit(solution)/shard_map/broadcast_in_dim | solution.py:447
  3.0 1.4 %copy.176.regb = f32[2,80,1]{2,1,0:T(8,128)} copy(f32[2,80,1]{1,0,2:T(2,128)} %bitcast.141) | data formatting | bytes 1280 | tf_op jit(solution)/shard_map/broadcast_in_dim | solution.py:447
  4.4 1.4 %copy.177.liftb = f32[192,1]{1,0:T(8,128)} copy(f32[192,1]{0,1:T(1,128)} %bitcast.137) | data formatting | bytes 1536 | tf_op jit(solution)/shard_map/broadcast_in_dim | solution.py:448
  5.8 1.5 %copy.178.midg = f32[192,1]{1,0:T(8,128)} copy(f32[192,1]{0,1:T(1,128)} %bitcast.138) | data formatting | bytes 1536 | tf_op jit(solution)/shard_map/broadcast_in_dim | solution.py:448
  7.3 1.4 %copy.180.midb = f32[192,1]{1,0:T(8,128)} copy(f32[192,1]{0,1:T(1,128)} %bitcast.139) | data formatting | bytes 1536 | tf_op jit(solution)/shard_map/broadcast_in_dim | solution.py:448
  8.7 1.0 %reshape.45 = bf16[80,2,4,128]{3,2,1,0:T(4,128)(2,1)S(1)} reshape(bf16[80,2,512]{2,1,0:T(2,128)(2,1)} %param.10) | data formatting | bytes 327680 | tf_op jit(solution)/shard_map/reshape | solution.py:403
  9.8 0.2 copy.172
  10.1 0.8 maximum_bitcast_fusion.1.pieces
  10.9 0.2 copy.158
  11.1 0.9 copy.175.regw
  12.0 0.3 copy.171
  12.2 0.4 maximum_maximum_fusion.1
  12.6 0.8 copy.183
  13.4 0.3 copy.153
  13.8 0.6 pad.59.cols
  14.4 0.7 copy.173
  15.1 1.1 %copy.179.midw = bf16[192,1728]{1,0:T(8,128)(2,1)} copy(bf16[192,1728]{0,1:T(8,128)(2,1)S(1)} %bitcast.126) | data formatting | bytes 1327104 | tf_op jit(solution)/shard_map/reshape | solution.py:443
  16.3 0.5 fusion.36
  16.8 0.3 copy.156
  17.1 0.3 copy.157
  17.5 0.6 reshape.37.rows
  18.1 14.6 %shard_map.100 = (bf16[8,2,80,256]{3,2,1,0:T(8,128)(2,1)}, bf16[6,16,128]{2,1,0:T(8,128)(2,1)}, bf16[2,16,512]{2,1,0:T(8,128)(2,1)}) custom-call(bf16[4,2,80,256]{3,2,1,0:T(8,128)(2,1)} %maximum_bitcast_fusion.1.pieces, bf16[16,128]{1,0:T(8,128)(2,1)} %pad.59.cols, bf16[16,512]{1,0:T(8,128)(2,1)} %reshape.37.rows), custom_call_target="tpu_custom_call" | custom-call | tf_op jit(solution)/shard_map/pallas_call | solution.py:135
  32.7 0.7 copy.185
  33.5 0.1 slice.207
  33.6 0.1 copy.160
  33.7 0.1 copy.165
  33.8 0.1 copy.163
  34.0 0.1 slice.210
  34.1 0.1 copy.162
  34.2 0.7 fusion.40
  35.0 0.1 maximum_select_fusion.1
  35.1 0.1 maximum_select_fusion.2
  35.2 0.4 copy.167
  35.6 0.4 copy.166
  36.0 1.2 %maximum_bitcast_fusion = bf16[36,4,516]{0,1,2:T(4,128)(2,1)S(1)} fusion(bf16[4,2,516]{1,0,2:T(4,128)(2,1)S(1)} %copy.167, bf16[4,32,2]{1,0,2:T(4,128)(2,1)S(1)} %slice.214, bf16[4,32,512]{1,0,2:T(4,128)(2,1)S(1)} %bitcast.125, bf16[4,32,2]{1,0,2:T(4,128)(2,1)S(1)} %slice.212, bf16[4,2,516]{1,0,2:T(4,128)(2,1)S(1)} %copy.166), kind=kLoop, calls=%fused_computation.1 | loop fusion | flops 743040 | bytes 297216 | tf_op jit(solution)/shard_map/transpose | solution.py:425
  37.1 0.1 slice_bitcast_fusion.24
  37.2 0.1 fusion.24
  37.3 0.6 pad_maximum_fusion.1.noise_edge
  37.9 0.4 fusion.35
  38.3 0.4 copy.168
  38.7 0.4 copy.170
  39.1 0.4 copy.169
  39.4 1.1 %maximum_maximum_fusion.noise = bf16[36,16,512]{2,1,0:T(8,128)(2,1)} fusion(bf16[36,4,512]{2,1,0:T(4,128)(2,1)S(1)} %copy.170, bf16[36,4,512]{2,1,0:T(4,128)(2,1)S(1)} %copy.169, bf16[36,4,512]{2,1,0:T(4,128)(2,1)S(1)} %copy.168, bf16[16]{0:T(256)(128)(2,1)S(1)} %pad.108.clone), kind=kLoop, calls=%fused_computation | loop fusion | flops 2359296 | bytes 1032224 | tf_op jit(solution)/shard_map/concatenate | solution.py:427
  40.5 50.4 %shard_map.101 = bf16[1,192,32,512]{3,2,1,0:T(8,128)(2,1)} custom-call(s32[2]{0:T(128)} %pad_add_fusion.info, bf16[16,80,256]{2,1,0:T(8,128)(2,1)} %bitcast.132, f32[2,80,1]{2,1,0:T(8,128)} %copy.174.gain, bf16[2,80,720]{2,1,0:T(8,128)(2,1)} %copy.175.regw, f32[2,80,1]{2,1,0:T(8,128)} %copy.176.regb, bf16[36,16,512]{2,1,0:T(8,128)(2,1)} %maximum_maximum_fusion.noise, ...), custom_call_target="tpu_custom_call" | custom-call | tf_op jit(solution)/shard_map/pallas_call | solution.py:368
  (31 shorter events, 0.3 us)
Async XLA Ops:
  9.8 1.1 %copy-start.1 = (bf16[2,3,3,80,80]{4,3,2,1,0:T(8,128)(2,1)S(1)}, bf16[2,3,3,80,80]{4,3,2,1,0:T(8,128)(2,1)}, u32[]{:S(2)}) copy-start(bf16[2,3,3,80,80]{4,3,2,1,0:T(8,128)(2,1)} %param.12) | copy-start | bytes 691204
  10.9 1.1 %slice-start = ((bf16[3,3,192,84]{2,3,1,0:T(8,128)(2,1)}), bf16[3,3,192,80]{2,3,1,0:T(8,128)(2,1)S(1)}, s32[]{:S(2)}) async-start(bf16[3,3,192,84]{2,3,1,0:T(8,128)(2,1)} %param.15), calls=%async_computation | async-start | bytes 737280 | tf_op jit(solution)/shard_map/slice | solution.py:440
  12.0 1.5 %copy-start.2 = (bf16[1,4,32,512]{3,2,1,0:T(8,128)(2,1)S(1)}, bf16[1,4,32,512]{3,2,1,0:T(8,128)(2,1)}, u32[]{:S(2)}) copy-start(bf16[1,4,32,512]{3,2,1,0:T(8,128)(2,1)} %param.14) | copy-start | bytes 393220
  12.2 2.2 %copy-start = (bf16[3,3,192,192]{3,2,1,0:T(8,128)(2,1)S(1)}, bf16[3,3,192,192]{3,2,1,0:T(8,128)(2,1)}, u32[]{:S(2)}) copy-start(bf16[3,3,192,192]{3,2,1,0:T(8,128)(2,1)} %param.18) | copy-start | bytes 1990660

commit v2 on v1

--- a/solution.py
+++ b/solution.py
@@ -146,13 +146,10 @@
     )(pieces, cols, rows)
 
 
-def silu(values):
-    return 0.5 * values * (1.0 + jnp.tanh(0.5 * values))
-
-
-def activate(values, gain):
+def activate(values, half_gain):
     inverse = lax.rsqrt(jnp.mean(values * values, axis=0, keepdims=True) + EPSILON)
-    return silu(values * inverse * gain)
+    half = values * inverse * half_gain
+    return half + half * jnp.tanh(half)
 
 
 def split(numerator, factor):
@@ -160,17 +157,28 @@
     return lower, (numerator - 2 * factor * lower).astype(F32) / (2.0 * factor)
 
 
+def column(row):
+    n = row.shape[1]
+    here = lax.broadcasted_iota(jnp.int32, (n, n), 0) == lax.broadcasted_iota(jnp.int32, (n, n), 1)
+    return jnp.broadcast_to(jnp.sum(jnp.where(here, row, 0.0), axis=1, keepdims=True), (n, 128))
+
+
 def tile_kernel(
     dims, info, got, gain, regw, regb, noise, noise_edge, liftw, liftb, midg, midw, midb, out,
-    taps, field, lon, lines, upper, sides, bands, keep, rows_out, stage, sems,
+    taps, field, lon, lines, upper, sides, bands, keep, raw, prod, edges, cols, rows_out, stage, sems,
 ):
     cin, ch, ct, fr, fl = dims
     bands_n = got.shape[0]
     cw = got.shape[2]
-    ccols = fl // LON_UP
     tile_row, tile_rows = info[0], info[1]
     top, bottom = tile_row == 0, tile_row == tile_rows - 1
     spare = (bands_n - ct) // 2
+    steps = bands.shape[0]
+    wide = fl // 128
+
+    cols[0] = column(liftb[...])
+    cols[1] = column(midg[...]) * 0.5
+    cols[2] = column(midb[...])
 
     def real(i):
         row = tile_row * ct - spare + i
@@ -179,46 +187,44 @@
     blocks = regw.shape[0]
     for k in range(blocks):
         first, last = 1 + k, bands_n - 1 - k
-
-        def fill(i, _, k=k):
+        half_gain = column(gain[k:k + 1, :])[:, :1] * 0.5
+        bias = column(regb[k:k + 1, :])[:, :1]
+
+        def fill(i, _, k=k, half_gain=half_gain):
             source = got[i] if k == 0 else field[i]
-            values = jnp.where(real(i), source.astype(F32), 0.0)
-            values = jnp.where(real(i), activate(values, gain[k]), 0.0)
+            values = activate(jnp.where(real(i), source.astype(F32), 0.0), half_gain)
             base = pl.multiple_of(i * 3 * cin, 16)
             taps[pl.ds(base, cin), :] = pltpu.roll(values, 1, 1).astype(BF16)
             taps[pl.ds(base + cin, cin), :] = values.astype(BF16)
             taps[pl.ds(base + 2 * cin, cin), :] = pltpu.roll(values, cw - 1, 1).astype(BF16)
             return 0
 
-        lax.fori_loop(first, last, fill, 0)
-
-        def conv(i, _, k=k):
+        lax.fori_loop(first, last, fill, 0, unroll=2)
+
+        def conv(i, _, k=k, bias=bias):
             base = pl.multiple_of((i - 1) * 3 * cin, 16)
             update = jnp.dot(regw[k], taps[pl.ds(base, 9 * cin), :], preferred_element_type=F32)
             source = got[i] if k == 0 else field[i]
-            field[i] = jnp.where(real(i), source.astype(F32) + update + regb[k], 0.0).astype(BF16)
+            field[i] = jnp.where(real(i), source.astype(F32) + update + bias, 0.0).astype(BF16)
             return 0
 
-        lax.fori_loop(first + 1, last - 1, conv, 0)
+        lax.fori_loop(first + 1, last - 1, conv, 0, unroll=2)
 
     first = 1 + blocks
     count = bands_n - 2 * first
+
+    def lon_split(fine_col):
+        lower, part = split(2 * fine_col + 1 - LON_UP + 2 * LON_UP, LON_UP)
+        return lower - 1, part
+
+    position = lax.broadcasted_iota(jnp.int32, (1, 3 * fl), 1)
+    shift = jnp.where(position >= 2 * fl, 2, jnp.where(position >= fl, 1, 0))
+    lower, part = lon_split(position - shift * fl + shift - 1)
+    low_lane = jnp.where(lower < 0, lower + cw, lower)
+    high_lane = jnp.where(lower + 1 < 0, lower + 1 + cw, lower + 1)
     coarse_lane = lax.broadcasted_iota(jnp.int32, (cw, 3 * fl), 0)
-    position = lax.broadcasted_iota(jnp.int32, (cw, 3 * fl), 1)
-
-    def lon_weights(fine_col, lane):
-        lower, part = split(2 * fine_col + 1 - LON_UP, LON_UP)
-        low_lane = jnp.where(lower < 0, lower + cw, lower)
-        high_lane = jnp.where(lower + 1 < 0, lower + 1 + cw, lower + 1)
-        return (jnp.where(lane == low_lane, 1.0 - part, 0.0)
-                + jnp.where(lane == high_lane, part, 0.0)).astype(BF16)
-
-    shift = jnp.where(position >= 2 * fl, 2, jnp.where(position >= fl, 1, 0))
-    lon[...] = lon_weights(position - shift * fl + shift - 1, coarse_lane)
-    edge_lane = lax.broadcasted_iota(jnp.int32, (cw, 128), 0)
-    edge_pos = lax.broadcasted_iota(jnp.int32, (cw, 128), 1)
-    edge_col = jnp.where(edge_pos < 3, edge_pos - 2, fl - 4 + edge_pos)
-    edge_weights = lon_weights(edge_col, edge_lane)
+    lon[...] = jnp.where(coarse_lane == low_lane, 1.0 - part,
+                         jnp.where(coarse_lane == high_lane, part, 0.0)).astype(BF16)
 
     def widen(i, _):
         for q in range(3):
@@ -226,7 +232,7 @@
                 field[i + first], lon[:, q * fl:(q + 1) * fl], preferred_element_type=F32)
         return 0
 
-    lax.fori_loop(0, count, widen, 0)
+    lax.fori_loop(0, count, widen, 0, unroll=2)
 
     low_line = jnp.where(top, 1, 0)
     high_line = jnp.where(bottom, count - 2, count - 1)
@@ -236,76 +242,102 @@
         row = tile_row * fr + t - 2
         return jnp.logical_and(row >= 0, row < fine_total)
 
-    slab = 3 * cin + noise.shape[1]
-
-    def raise_row(t):
+    def lat_split(t):
         lower, part = split(2 * (t - 2) + 1 - LAT_UP + 2 * LAT_UP, LAT_UP)
-        a = jnp.clip(lower, low_line, high_line)
-        b = jnp.clip(lower + 1, low_line, high_line)
-        blended = (1.0 - part) * lines[a] + part * lines[b]
-        base = pl.multiple_of(t * slab, 16)
-        upper[pl.ds(base, 3 * cin), :] = jnp.where(inside(t), blended, 0.0).astype(BF16)
-        upper[pl.ds(base + 3 * cin, noise.shape[1]), :] = noise[t]
+        return jnp.clip(lower, low_line, high_line), jnp.clip(lower + 1, low_line, high_line), part
+
+    nrows = noise.shape[1]
+    slab = 3 * cin + nrows
+
+    def raise_row(t, slot):
+        a, b, part = lat_split(t)
+        ok = inside(t)
+        wa = jnp.where(ok, 1.0 - part, 0.0)
+        wb = jnp.where(ok, part, 0.0)
+        for o in range(0, 3 * cin, 16):
+            upper[slot, o:o + 16, :] = (wa * lines[a, o:o + 16, :] + wb * lines[b, o:o + 16, :]).astype(BF16)
+        upper[slot, 3 * cin:slab, :] = noise[t]
 
     lane = lax.broadcasted_iota(jnp.int32, (1, 128), 1)
-    left = lane < HALF
-    edge_row = jnp.where(left, lane, lane - HALF)
-    sums = [[jnp.zeros((cin, 128), F32) for _ in range(3)] for _ in range(3)]
-    weights = []
+    edge_row = jnp.where(lane < HALF, lane, lane - HALF)
+    near = fl // LON_UP
+    picked_cols = [-1, 0, near - 1, near]
+    select_lane = lax.broadcasted_iota(jnp.int32, (cw, 128), 0)
+    select_pos = lax.broadcasted_iota(jnp.int32, (cw, 128), 1)
+    hits = jnp.zeros((cw, 128), jnp.bool_)
+    for s, col in enumerate(picked_cols):
+        hits = jnp.logical_or(hits, jnp.logical_and(select_pos == s, select_lane == col % cw))
+    chosen = jnp.where(hits, 1.0, 0.0).astype(BF16)
+    packed = jnp.zeros((cin, 128), F32)
+    for i in range(count):
+        narrow = jnp.dot(field[first + i], chosen, preferred_element_type=F32)
+        packed = packed + (pltpu.roll(narrow, 4 * i, 1) if i else narrow)
+    packed = packed.astype(BF16)
+    key = lax.broadcasted_iota(jnp.int32, (128, 1), 0)
+    key_line = key // 4
+    key_pick = key - 4 * key_line
+    key_col = jnp.where(key_pick == 0, picked_cols[0], jnp.where(
+        key_pick == 1, picked_cols[1], jnp.where(key_pick == 2, picked_cols[2], picked_cols[3])))
     for p in range(3):
         t = edge_row + p
-        lower, part = split(2 * (t - 2) + 1 - LAT_UP + 2 * LAT_UP, LAT_UP)
-        a = jnp.clip(lower, low_line, high_line)
-        b = jnp.clip(lower + 1, low_line, high_line)
+        a, b, part = lat_split(t)
         ok = inside(t)
-        weights.append([jnp.where(ok, jnp.where(a == i, 1.0 - part, 0.0) + jnp.where(b == i, part, 0.0), 0.0)
-                        for i in range(count)])
-    for i in range(count):
-        narrow = jnp.dot(field[first + i], edge_weights, preferred_element_type=F32)
+        wa = jnp.where(ok, 1.0 - part, 0.0)
+        wb = jnp.where(ok, part, 0.0)
+        by_row = jnp.where(key_line == a, wa, 0.0) + jnp.where(key_line == b, wb, 0.0)
         for q in range(3):
-            column = jnp.where(left, narrow[:, q:q + 1], narrow[:, 3 + q:4 + q])
-            for p in range(3):
-                sums[p][q] = sums[p][q] + weights[p][i] * column
-    for p in range(3):
-        for q in range(3):
+            lower, part_m = lon_split(jnp.where(lane < HALF, q - 2, fl - 1 + q))
+            by_col = jnp.where(key_col == lower, 1.0 - part_m, jnp.where(key_col == lower + 1, part_m, 0.0))
             base = p * slab + q * cin
-            sides[base:base + cin, :] = sums[p][q].astype(BF16)
+            sides[base:base + cin, :] = jnp.dot(
+                packed, (by_row * by_col).astype(BF16), preferred_element_type=F32).astype(BF16)
         sides[p * slab + 3 * cin:(p + 1) * slab, :] = noise_edge[p]
-    edge_lift = jnp.dot(liftw[...], sides[...], preferred_element_type=F32) + liftb[...]
+    edge_lift = jnp.dot(liftw[...], sides[...], preferred_element_type=F32) + cols[0]
     edge_lift = edge_lift.astype(BF16).astype(F32)
-    edge_act = jnp.where(inside(edge_row + 1), activate(edge_lift, midg[...]), 0.0)
-
-    for t in range(3):
-        raise_row(jnp.int32(t))
-
-    lane_full = lax.broadcasted_iota(jnp.int32, (1, fl), 1)
-    kept = keep.shape[0]
+    edges[...] = jnp.where(inside(edge_row + 1), activate(edge_lift, cols[1]), 0.0)
+
+    lane_first, lane_last = lane == 0, lane == 127
+
+    def lift(slot):
+        window = jnp.concatenate([upper[(slot + n) % steps] for n in range(3)], axis=0)
+        raw[slot % 2] = jnp.dot(liftw[...], window, preferred_element_type=F32)
+
+    def finish(l, slot):
+        squares = jnp.zeros((8, fl), F32)
+        for o in range(0, ch, 16):
+            bias = jnp.concatenate([cols[0, o:o + 16, :]] * wide, axis=1)
+            rounded = (raw[slot % 2, o:o + 16, :] + bias).astype(BF16)
+            keep[slot, o:o + 16, :] = rounded
+            values = rounded.astype(F32)
+            values = values * values
+            squares = squares + (values[:8] + values[8:])
+        inverse = lax.rsqrt(jnp.sum(squares, axis=0, keepdims=True) * (1.0 / ch) + EPSILON)
+        inverse = jnp.where(inside(l + 1), inverse, 0.0)
+        for o in range(0, ch, 16):
+            half_gain = jnp.concatenate([cols[1, o:o + 16, :]] * wide, axis=1)
+            half = keep[slot, o:o + 16, :].astype(F32) * inverse * half_gain
+            values = half + half * jnp.tanh(half)
+            edge = edges[o:o + 16, :]
+            parts = [values[:, j * 128:(j + 1) * 128] for j in range(wide)]
+            east = [pltpu.roll(v, 1, 1) for v in parts]
+            west = [pltpu.roll(v, 127, 1) for v in parts]
+            edge_l = pltpu.roll(edge, 128 - l, 1)
+            edge_r = pltpu.roll(edge, 128 + HALF - 1 - l, 1)
+            bands[slot, ch + o:ch + o + 16, :] = values.astype(BF16)
+            bands[slot, o:o + 16, :] = jnp.concatenate(
+                [jnp.where(lane_first, east[j - 1] if j else edge_l, east[j]) for j in range(wide)],
+                axis=1).astype(BF16)
+            bands[slot, 2 * ch + o:2 * ch + o + 16, :] = jnp.concatenate(
+                [jnp.where(lane_last, west[j + 1] if j < wide - 1 else edge_r, west[j]) for j in range(wide)],
+                axis=1).astype(BF16)
+
+    def mid(slot):
+        window = jnp.concatenate([bands[(slot + n) % steps] for n in range(3)], axis=0)
+        prod[slot % 2] = jnp.dot(midw[...], window, preferred_element_type=F32)
+
     group = stage.shape[2]
 
-    def lift(l):
-        base = pl.multiple_of(l * slab, 16)
-        return jnp.dot(liftw[...], upper[pl.ds(base, 3 * slab), :], preferred_element_type=F32) + liftb[...]
-
-    def finish(l, lifted):
-        rounded = lifted.astype(BF16)
-        keep[l % kept] = rounded
-        values = jnp.where(inside(l + 1), activate(rounded.astype(F32), midg[...]), 0.0)
-        turned = pltpu.roll(edge_act, 128 - l, 1)
-        edge_l = jnp.concatenate([turned[:, :128]] + [turned] * (fl // 128 - 1), axis=1)
-        turned_r = pltpu.roll(edge_act, HALF - 1 - l + 128, 1)
-        edge_r = jnp.concatenate([turned_r] * (fl // 128), axis=1)
-        base = pl.multiple_of(l * 3 * ch, 16)
-        bands[pl.ds(base, ch), :] = jnp.where(lane_full == 0, edge_l, pltpu.roll(values, 1, 1)).astype(BF16)
-        bands[pl.ds(base + ch, ch), :] = values.astype(BF16)
-        bands[pl.ds(base + 2 * ch, ch), :] = jnp.where(
-            lane_full == fl - 1, edge_r, pltpu.roll(values, fl - 1, 1)).astype(BF16)
-
-    def mid(y):
-        base = pl.multiple_of(y * 3 * ch, 16)
-        return jnp.dot(midw[...], bands[pl.ds(base, 9 * ch), :], preferred_element_type=F32)
-
-    def flush(y):
-        part = y // group
+    def flush(part):
         slot = part % 2
 
         def copy(n):
@@ -317,7 +349,7 @@
             copy(part - 2).wait()
 
         def shrink(o, _):
-            for j in range(fl // 128):
+            for j in range(wide):
                 block = rows_out[j, pl.ds(pl.multiple_of(o * 8 * group, 8 * group), 8 * group), :]
                 stage[slot, pl.ds(o * 8, 8), :, j * 128:(j + 1) * 128] = block.reshape(8, group, 128).astype(BF16)
             return 0
@@ -325,33 +357,38 @@
         lax.fori_loop(0, ch // 8, shrink, 0)
         copy(part).start()
 
-    def emit(y, product):
-        total = keep[(y + 1) % kept].astype(F32) + product + midb[...]
-        for j in range(fl // 128):
-            rows_out[j, pl.ds(y % group, ch, stride=group), :] = total[:, j * 128:(j + 1) * 128]
-
-        @pl.when(y % group == group - 1)
+    def emit(y, slot):
+        spot = y % group
+        for o in range(0, ch, 16):
+            bias = cols[2, o:o + 16, :]
+            for j in range(wide):
+                at = slice(j * 128, (j + 1) * 128)
+                total = keep[(slot + 1) % steps, o:o + 16, at].astype(F32) + prod[slot % 2, o:o + 16, at] + bias
+                rows_out[j, pl.ds(spot + o * group, 16, stride=group), :] = total
+
+    for t in range(3):
+        raise_row(jnp.int32(t), t % steps)
+    for l in range(3):
+        lift(l % steps)
+        raise_row(jnp.int32(l + 3), (l + 3) % steps)
+        finish(jnp.int32(l), l % steps)
+
+    def trip(i, _):
+        for j in range(steps):
+            l = i * steps + j + 3
+            slot = (j + 3) % steps
+            lift(slot)
+            mid(j)
+            raise_row(jnp.minimum(l + 3, fr + 3), (j + 6) % steps)
+            finish(l, slot)
+            emit(l - 3, j)
+
+        @pl.when((i + 1) % (group // steps) == 0)
         def _():
-            flush(y)
-
-    def lead(l, _):
-        lifted = lift(l)
-        raise_row(l + 3)
-        finish(l, lifted)
+            flush(i // (group // steps))
         return 0
 
-    lax.fori_loop(0, 3, lead, 0)
-
-    def both(l, _):
-        lifted = lift(l)
-        product = mid(l - 3)
-        raise_row(jnp.minimum(l + 3, fr + 3))
-        finish(l, lifted)
-        emit(l - 3, product)
-        return 0
-
-    lax.fori_loop(3, fr + 2, both, 0)
-    emit(fr - 1, mid(fr - 1))
+    lax.fori_loop(0, fr // steps, trip, 0)
     parts = fr // group
     for n in range(max(parts - 2, 0), parts):
         pltpu.make_async_copy(stage.at[n % 2], out.at[0, :, pl.ds(n * group, group), :], sems.at[n % 2]).wait()
@@ -363,6 +400,7 @@
     fr, fl = noise.shape[0] - 4, noise.shape[2]
     count = ct + 2
     group = 16
+    steps = 4
     vmem = pl.BlockSpec(memory_space=pltpu.VMEM)
     slab = 3 * cin + noise.shape[1]
     return pl.pallas_call(
@@ -375,15 +413,19 @@
             pltpu.VMEM(got.shape, BF16),
             pltpu.VMEM((cw, 3 * fl), BF16),
             pltpu.VMEM((count, 3 * cin, fl), F32),
-            pltpu.VMEM(((fr + 4) * slab, fl), BF16),
+            pltpu.VMEM((steps, slab, fl), BF16),
             pltpu.VMEM((3 * slab, 128), BF16),
-            pltpu.VMEM(((fr + 2) * 3 * ch, fl), BF16),
-            pltpu.VMEM((8, ch, fl), BF16),
+            pltpu.VMEM((steps, 3 * ch, fl), BF16),
+            pltpu.VMEM((steps, ch, fl), BF16),
+            pltpu.VMEM((2, ch, fl), F32),
+            pltpu.VMEM((2, ch, fl), F32),
+            pltpu.VMEM((ch, 128), F32),
+            pltpu.VMEM((3, ch, 128), F32),
             pltpu.VMEM((fl // 128, ch * group, 128), F32),
             pltpu.VMEM((2, ch, group, fl), BF16),
             pltpu.SemaphoreType.DMA((2,)),
         ],
-        compiler_params=pltpu.CompilerParams(vmem_limit_bytes=66_000_000),
+        compiler_params=pltpu.CompilerParams(vmem_limit_bytes=60_000_000),
     )(info, got, gain, regw, regb, noise, noise_edge, liftw, liftb, midg, midw, midb)
 
 
@@ -444,8 +486,8 @@
     info = jnp.stack([tile_row, jnp.int32(tile_rows)]).astype(jnp.int32)
     got = got.reshape((got.shape[0] * band_rows,) + got.shape[2:])
     return tile_program(
-        info, got, reg_gain[:, :, None], regw, reg_bias[:, :, None], noise, noise_edge,
-        liftw, lift_bias[:, None], mid_gain[:, None], midw, mid_bias[:, None], ct)
+        info, got, reg_gain, regw, reg_bias, noise, noise_edge,
+        liftw, lift_bias[None], mid_gain[None], midw, mid_bias[None], ct)
 
 
 def solution(mesh):

time: 91.5 us -> 73 us (0.80)
  Pallas kernels: 65 us -> 53.7 us
  local copies, waits for them, and re-layouts: 20.7 us -> 13.5 us
    pallas_call x1, Pallas kernels: 50.4 us -> 39.1 us  [tile_program(): pl.pallas_call(functools.partial(tile_kernel, (cin, ch, ct, fr, fl)), out...]
    broadcast_in_dim x5 -> x0, local copies, waits for them, and re-layouts: 7.18 us -> none  [the longest x1 1.45 us: per_device(): mid_gain[:, None]]
where the time goes in v2:
time: 73 us; the launch traced here: 72.7 us
  Pallas kernels  53.7 us (74%)
  local copies, waits for them, and re-layouts  13.5 us (18%)
  other arithmetic  5.06 us (7%)
    pallas_call x1, Pallas kernels, tile_program(): pl.pallas_call(functools.partial(tile_kernel, (cin, ch, ct, fr, fl)), out...  39.1 us
    pallas_call x1, Pallas kernels, gather(): pl.pallas_call(gather_kernel, out_shape=(jax.ShapeDtypeStruct((8,) + piec...  14.6 us
    slice x4, local copies, waits for them, and re-layouts, per_device(): whole[:, :, 1 + q:1 + q + fl]  1.48 us

profile of v2, /device:TPU:0, one launch (start us, length us, event | category | flops | bytes accessed | tf_op | source)
XLA Modules:
  0.0 72.7 jit_solution(13111912626955640239)
XLA Ops:
  0.0 0.7 pad_add_fusion.info
  0.7 0.1 pad.108.clone
  0.7 0.1 pad.80.clone
  0.8 0.8 %slice_bitcast_fusion = bf16[192,3,3,4]{0,3,2,1:T(4,128)(2,1)S(1)} fusion(bf16[3,3,192,84]{2,3,1,0:T(8,128)(2,1)} %param.15), kind=kLoop, calls=%fused_computation.6 | loop fusion | bytes 27648 | tf_op jit(solution)/shard_map/transpose | solution.py:483
  1.6 1.0 %reshape.45 = bf16[80,2,4,128]{3,2,1,0:T(4,128)(2,1)S(1)} reshape(bf16[80,2,512]{2,1,0:T(2,128)(2,1)} %param.10) | data formatting | bytes 327680 | tf_op jit(solution)/shard_map/reshape | solution.py:445
  2.7 0.0 copy-start.1
  2.7 0.2 copy.152
  3.0 0.8 %maximum_bitcast_fusion.1.pieces = bf16[4,2,80,256]{3,2,1,0:T(8,128)(2,1)} fusion(bf16[80,2,4,128]{3,0,1,2:T(8,128)(2,1)S(1)} %maximum_select_fusion, bf16[80,2,4,128]{3,0,1,2:T(8,128)(2,1)S(1)} %copy.132), kind=kLoop, calls=%fused_computation.3 | loop fusion | flops 655360 | bytes 655360 | tf_op jit(solution)/shard_map/transpose | solution.py:449
  3.7 0.0 copy-done.1
  3.8 0.2 copy.138
  4.0 0.9 %copy.154.regw = bf16[2,80,720]{2,1,0:T(8,128)(2,1)} copy(bf16[2,80,720]{1,2,0:T(8,128)(2,1)S(1)} %bitcast.126) | data formatting | bytes 460800 | tf_op jit(solution)/shard_map/reshape | solution.py:481
  4.8 0.0 slice-done
  4.9 0.3 copy.151
  5.1 0.0 copy-start
  5.1 0.4 maximum_maximum_fusion.1
  5.5 0.8 %copy.158 = bf16[24,8,3,256]{3,1,2,0:T(8,128)(2,1)} copy(bf16[24,8,3,256]{3,2,1,0:T(4,128)(2,1)S(1)} %bitcast.125) | data formatting | bytes 589824
  6.3 0.0 copy-done.2
  6.3 0.3 copy.133
  6.7 0.6 pad.59.cols
  7.3 0.7 %copy.153 = bf16[192,3,3,192]{0,3,2,1:T(8,128)(2,1)S(1)} copy(bf16[192,3,3,192]{3,0,2,1:T(8,128)(2,1)S(1)} %bitcast.129) | data formatting | bytes 1327104 | tf_op jit(solution)/shard_map/transpose | solution.py:485
  8.0 1.1 %copy.155.midw = bf16[192,1728]{1,0:T(8,128)(2,1)} copy(bf16[192,1728]{0,1:T(8,128)(2,1)S(1)} %bitcast.124) | data formatting | bytes 1327104 | tf_op jit(solution)/shard_map/reshape | solution.py:485
  9.2 0.5 fusion.36
  9.7 0.3 copy.136
  10.0 0.3 copy.137
  10.4 0.6 reshape.37.rows
  11.0 14.6 %shard_map.100 = (bf16[8,2,80,256]{3,2,1,0:T(8,128)(2,1)}, bf16[6,16,128]{2,1,0:T(8,128)(2,1)}, bf16[2,16,512]{2,1,0:T(8,128)(2,1)}) custom-call(bf16[4,2,80,256]{3,2,1,0:T(8,128)(2,1)} %maximum_bitcast_fusion.1.pieces, bf16[16,128]{1,0:T(8,128)(2,1)} %pad.59.cols, bf16[16,512]{1,0:T(8,128)(2,1)} %reshape.37.rows), custom_call_target="tpu_custom_call" | custom-call | tf_op jit(solution)/shard_map/pallas_call | solution.py:135
  25.6 0.7 %copy.160 = bf16[6,4,4,32]{3,1,2,0:T(4,128)(2,1)S(1)} copy(bf16[6,4,4,32]{3,2,1,0:T(4,128)(2,1)} %bitcast.133) | data formatting | bytes 12288 | tf_op jit(solution)/shard_map/reshape | solution.py:461
  26.4 0.1 slice.207
  26.5 0.1 copy.140
  26.6 0.1 copy.145
  26.7 0.1 copy.143
  26.9 0.1 slice.210
  27.0 0.1 copy.142
  27.1 0.7 %fusion.40 = (bf16[1,16,512]{2,1,0:T(8,128)(2,1)S(1)}, bf16[1,16,512]{2,1,0:T(8,128)(2,1)S(1)}) fusion(bf16[2,16,512]{2,1,0:T(8,128)(2,1)} %get-tuple-element.10), kind=kLoop, calls=%fused_computation.91 | loop fusion | bytes 65536 | tf_op jit(solution)/shard_map/slice | solution.py:464
  27.9 0.1 maximum_select_fusion.1
  28.0 0.1 maximum_select_fusion.2
  28.1 0.4 copy.147
  28.5 0.4 copy.146
  28.9 1.2 %maximum_bitcast_fusion = bf16[36,4,516]{0,1,2:T(4,128)(2,1)S(1)} fusion(bf16[4,2,516]{1,0,2:T(4,128)(2,1)S(1)} %copy.147, bf16[4,32,2]{1,0,2:T(4,128)(2,1)S(1)} %slice.214, bf16[4,32,512]{1,0,2:T(4,128)(2,1)S(1)} %bitcast.123, bf16[4,32,2]{1,0,2:T(4,128)(2,1)S(1)} %slice.212, bf16[4,2,516]{1,0,2:T(4,128)(2,1)S(1)} %copy.146), kind=kLoop, calls=%fused_computation.1 | loop fusion | flops 743040 | bytes 297216 | tf_op jit(solution)/shard_map/transpose | solution.py:467
  30.0 0.1 slice_bitcast_fusion.24
  30.1 0.1 fusion.24
  30.2 0.6 pad_maximum_fusion.1.noise_edge
  30.8 0.4 fusion.35
  31.2 0.4 copy.148
  31.6 0.4 copy.150
  32.0 0.4 copy.149
  32.3 1.1 %maximum_maximum_fusion.noise = bf16[36,16,512]{2,1,0:T(8,128)(2,1)} fusion(bf16[36,4,512]{2,1,0:T(4,128)(2,1)S(1)} %copy.150, bf16[36,4,512]{2,1,0:T(4,128)(2,1)S(1)} %copy.149, bf16[36,4,512]{2,1,0:T(4,128)(2,1)S(1)} %copy.148, bf16[16]{0:T(256)(128)(2,1)S(1)} %pad.108.clone), kind=kLoop, calls=%fused_computation | loop fusion | flops 2359296 | bytes 1032224 | tf_op jit(solution)/shard_map/concatenate | solution.py:469
  33.4 39.1 %shard_map.101 = bf16[1,192,32,512]{3,2,1,0:T(8,128)(2,1)} custom-call(s32[2]{0:T(128)} %pad_add_fusion.info, bf16[16,80,256]{2,1,0:T(8,128)(2,1)} %bitcast.130, f32[2,80]{1,0:T(2,128)} %gain.1, bf16[2,80,720]{2,1,0:T(8,128)(2,1)} %copy.154.regw, f32[2,80]{1,0:T(2,128)} %regb.1, bf16[36,16,512]{2,1,0:T(8,128)(2,1)} %maximum_maximum_fusion.noise, ...), custom_call_target="tpu_custom_call" | custom-call | tf_op jit(solution)/shard_map/pallas_call | solution.py:406
  (26 shorter events, 0.3 us)
Async XLA Ops:
  2.7 1.1 %copy-start.1 = (bf16[2,3,3,80,80]{4,3,2,1,0:T(8,128)(2,1)S(1)}, bf16[2,3,3,80,80]{4,3,2,1,0:T(8,128)(2,1)}, u32[]{:S(2)}) copy-start(bf16[2,3,3,80,80]{4,3,2,1,0:T(8,128)(2,1)} %param.12) | copy-start | bytes 691204
  3.8 1.1 %slice-start = ((bf16[3,3,192,84]{2,3,1,0:T(8,128)(2,1)}), bf16[3,3,192,80]{2,3,1,0:T(8,128)(2,1)S(1)}, s32[]{:S(2)}) async-start(bf16[3,3,192,84]{2,3,1,0:T(8,128)(2,1)} %param.15), calls=%async_computation | async-start | bytes 737280 | tf_op jit(solution)/shard_map/slice | solution.py:482
  4.9 1.5 %copy-start.2 = (bf16[1,4,32,512]{3,2,1,0:T(8,128)(2,1)S(1)}, bf16[1,4,32,512]{3,2,1,0:T(8,128)(2,1)}, u32[]{:S(2)}) copy-start(bf16[1,4,32,512]{3,2,1,0:T(8,128)(2,1)} %param.14) | copy-start | bytes 393220
  5.1 2.2 %copy-start = (bf16[3,3,192,192]{3,2,1,0:T(8,128)(2,1)S(1)}, bf16[3,3,192,192]{3,2,1,0:T(8,128)(2,1)}, u32[]{:S(2)}) copy-start(bf16[3,3,192,192]{3,2,1,0:T(8,128)(2,1)} %param.18) | copy-start | bytes 1990660

commit v3 on v2

--- a/solution.py
+++ b/solution.py
@@ -17,7 +17,10 @@
 HALF = 64
 
 
-def gather_kernel(pieces, cols, rows, got, got_cols, got_rows, send, recv, nsend, nrecv, local):
+def gather_kernel(
+    pieces, cols, rows, regs, lifts, mids, got, got_cols, got_rows, regw, liftw, midw,
+    send, recv, nsend, nrecv, local,
+):
     me = lax.axis_index("lat")
     tile_rows = lax.axis_size("lat") // TILE_COLS
     r = me // TILE_COLS
@@ -50,9 +53,11 @@
             src_ref=src, dst_ref=dst, send_sem=ssem, recv_sem=rsem,
             device_id={"lat": target}, device_id_type=MESH)
 
-    def band_copy(k, row, slot, ssem):
+    whole, upper, lower = pl.ds(0, 3), pl.ds(0, 2), pl.ds(1, 2)
+
+    def band_copy(k, row, slot, ssem, part=whole):
         col = (c + k) % TILE_COLS
-        return remote(pieces.at[col], got.at[slot], send.at[ssem], recv.at[slot], row * TILE_COLS + col)
+        return remote(pieces.at[col, part], got.at[slot, part], send.at[ssem], recv.at[slot], row * TILE_COLS + col)
 
     west, east = (c + TILE_COLS - 1) % TILE_COLS, (c + 1) % TILE_COLS
 
@@ -60,20 +65,17 @@
         return remote(cols, got_cols.at[slot], nsend.at[slot], nrecv.at[slot], row * TILE_COLS + col)
 
     def row_copy(slot, row):
-        return remote(rows, got_rows.at[slot], nsend.at[6 + slot], nrecv.at[6 + slot], row * TILE_COLS + c)
-
-    low, high = c < 2, c >= 2
+        return remote(rows, got_rows.at[slot], nsend.at[8 + slot], nrecv.at[8 + slot], row * TILE_COLS + c)
 
     def each(action):
-        @pl.when(jnp.logical_and(south, high))
-        def _():
-            for k in range(TILE_COLS):
-                action(band_copy(k, r + 1, c - 2, TILE_COLS + k))
-
-        @pl.when(jnp.logical_and(north, low))
-        def _():
-            for k in range(TILE_COLS):
-                action(band_copy(k, r - 1, 6 + c, TILE_COLS + k))
+        for col, side, row, slot, part in (
+            (2, south, r + 1, 0, lower), (3, south, r + 1, 1, whole),
+            (0, north, r - 1, 6, whole), (1, north, r - 1, 7, upper),
+        ):
+            @pl.when(jnp.logical_and(side, c == col))
+            def _():
+                for k in range(TILE_COLS):
+                    action(band_copy(k, row, slot, TILE_COLS + k, part))
 
         for k in range(1, TILE_COLS):
             action(band_copy(k, r, 2 + c, k))
@@ -83,29 +85,49 @@
         @pl.when(south)
         def _():
             action(row_copy(0, r + 1))
+            action(col_copy(6, r + 1, c))
             action(col_copy(2, r + 1, east))
             action(col_copy(3, r + 1, west))
 
         @pl.when(north)
         def _():
             action(row_copy(1, r - 1))
+            action(col_copy(7, r - 1, c))
             action(col_copy(4, r - 1, east))
             action(col_copy(5, r - 1, west))
 
     each(lambda copy: copy.start())
     own = pltpu.make_async_copy(pieces.at[c], got.at[2 + c], local)
     own.start()
+
+    cin, ch = regs.shape[2], mids.shape[1]
+    nout = lifts.shape[2] - cin
+    for k in range(regs.shape[0] // 9):
+        for tap in range(9):
+            regw[k, :, tap * cin:(tap + 1) * cin] = regs[9 * k + tap]
+    for tap in range(9):
+        midw[:, tap * ch:(tap + 1) * ch] = mids[tap]
+    slab = liftw.shape[1] // 3
+    for p in range(3):
+        for q in range(3):
+            base = p * slab + q * cin
+            liftw[:, base:base + cin] = lifts[3 * p + q, :, :cin]
+            base = p * slab + 3 * cin + q * nout
+            liftw[:, base:base + nout] = lifts[3 * p + q, :, cin:]
+        base = p * slab + 3 * (cin + nout)
+        liftw[:, base:(p + 1) * slab] = jnp.zeros((ch, (p + 1) * slab - base), BF16)
+
     own.wait()
     each(lambda copy: copy.wait_send())
 
-    def arrived(slot):
-        remote(pieces.at[0], got.at[slot], send.at[0], recv.at[slot], me).wait_recv()
+    def arrived(slot, part=whole):
+        remote(pieces.at[0, part], got.at[slot, part], send.at[0], recv.at[slot], me).wait_recv()
 
     def edge(slot):
-        if slot < 6:
+        if slot < 8:
             remote(cols, got_cols.at[slot], nsend.at[slot], nrecv.at[slot], me).wait_recv()
         else:
-            remote(rows, got_rows.at[slot - 6], nsend.at[slot], nrecv.at[slot], me).wait_recv()
+            remote(rows, got_rows.at[slot - 8], nsend.at[slot], nrecv.at[slot], me).wait_recv()
 
     for k in range(1, TILE_COLS):
         arrived(2 + (c + k) % TILE_COLS)
@@ -114,36 +136,39 @@
 
     @pl.when(north)
     def _():
-        arrived(0)
+        arrived(0, lower)
         arrived(1)
-        edge(2)
-        edge(3)
-        edge(6)
+        for slot in (2, 3, 6, 8):
+            edge(slot)
 
     @pl.when(south)
     def _():
         arrived(6)
-        arrived(7)
-        edge(4)
-        edge(5)
-        edge(7)
-
-
-def gather(pieces, cols, rows):
+        arrived(7, upper)
+        for slot in (4, 5, 7, 9):
+            edge(slot)
+
+
+def gather(pieces, cols, rows, regs, lifts, mids, slab):
     any_space = pl.BlockSpec(memory_space=pl.ANY)
+    vmem = pl.BlockSpec(memory_space=pltpu.VMEM)
     dma = pltpu.SemaphoreType.DMA
+    cin, ch = regs.shape[2], mids.shape[1]
     return pl.pallas_call(
         gather_kernel,
         out_shape=(
             jax.ShapeDtypeStruct((8,) + pieces.shape[1:], BF16),
-            jax.ShapeDtypeStruct((6,) + cols.shape, BF16),
+            jax.ShapeDtypeStruct((8,) + cols.shape, BF16),
             jax.ShapeDtypeStruct((2,) + rows.shape, BF16),
+            jax.ShapeDtypeStruct((regs.shape[0] // 9, cin, 9 * cin), BF16),
+            jax.ShapeDtypeStruct((ch, 3 * slab), BF16),
+            jax.ShapeDtypeStruct((ch, 9 * ch), BF16),
         ),
-        in_specs=[any_space] * 3,
-        out_specs=(any_space,) * 3,
-        scratch_shapes=[dma((2 * TILE_COLS,)), dma((8,)), dma((8,)), dma((8,)), dma],
+        in_specs=[any_space] * 3 + [vmem] * 3,
+        out_specs=(any_space,) * 3 + (vmem,) * 3,
+        scratch_shapes=[dma((2 * TILE_COLS,)), dma((8,)), dma((10,)), dma((10,)), dma],
         compiler_params=pltpu.CompilerParams(collective_id=0, has_side_effects=True),
-    )(pieces, cols, rows)
+    )(pieces, cols, rows, regs, lifts, mids)
 
 
 def activate(values, half_gain):
@@ -164,13 +189,13 @@
 
 
 def tile_kernel(
-    dims, info, got, gain, regw, regb, noise, noise_edge, liftw, liftb, midg, midw, midb, out,
-    taps, field, lon, lines, upper, sides, bands, keep, raw, prod, edges, cols, rows_out, stage, sems,
+    dims, got, gain, regw, regb, tile, own_cols, got_cols, got_rows, liftw, liftb, midg, midw, midb, out,
+    grid, taps, field, lon, lines, upper, sides, bands, keep, raw, prod, edges, cols, rows_out, stage, sems,
 ):
     cin, ch, ct, fr, fl = dims
-    bands_n = got.shape[0]
-    cw = got.shape[2]
-    tile_row, tile_rows = info[0], info[1]
+    bands_n, cw = field.shape[0], field.shape[2]
+    tile_row, tile_rows = lax.axis_index("lat") // TILE_COLS, lax.axis_size("lat") // TILE_COLS
+    nout = tile.shape[1]
     top, bottom = tile_row == 0, tile_row == tile_rows - 1
     spare = (bands_n - ct) // 2
     steps = bands.shape[0]
@@ -190,22 +215,37 @@
         half_gain = column(gain[k:k + 1, :])[:, :1] * 0.5
         bias = column(regb[k:k + 1, :])[:, :1]
 
-        def fill(i, _, k=k, half_gain=half_gain):
-            source = got[i] if k == 0 else field[i]
-            values = activate(jnp.where(real(i), source.astype(F32), 0.0), half_gain)
+        def fill(i, values, half_gain=half_gain):
+            values = activate(jnp.where(real(i), values, 0.0), half_gain)
             base = pl.multiple_of(i * 3 * cin, 16)
             taps[pl.ds(base, cin), :] = pltpu.roll(values, 1, 1).astype(BF16)
             taps[pl.ds(base + cin, cin), :] = values.astype(BF16)
             taps[pl.ds(base + 2 * cin, cin), :] = pltpu.roll(values, cw - 1, 1).astype(BF16)
+
+        def fill_first(n, _, fill=fill):
+            rims = got[n, 1].astype(F32)
+            turned = pltpu.roll(rims, cw // 4, 1)
+            for sub in range(2):
+                rim = jnp.where(lax.broadcasted_iota(jnp.int32, (1, cw // 2), 1) < cw // 8,
+                                turned if sub else rims, rims if sub else turned)
+                values = jnp.concatenate([got[n, 2 * sub].astype(F32), rim], axis=1)
+                field[2 * n + sub] = values.astype(BF16)
+                fill(2 * n + sub, values)
             return 0
 
-        lax.fori_loop(first, last, fill, 0, unroll=2)
+        def fill_next(i, _, fill=fill):
+            fill(i, field[i].astype(F32))
+            return 0
+
+        if k == 0:
+            lax.fori_loop(0, bands_n // 2, fill_first, 0)
+        else:
+            lax.fori_loop(first, last, fill_next, 0, unroll=2)
 
         def conv(i, _, k=k, bias=bias):
             base = pl.multiple_of((i - 1) * 3 * cin, 16)
             update = jnp.dot(regw[k], taps[pl.ds(base, 9 * cin), :], preferred_element_type=F32)
-            source = got[i] if k == 0 else field[i]
-            field[i] = jnp.where(real(i), source.astype(F32) + update + bias, 0.0).astype(BF16)
+            field[i] = jnp.where(real(i), field[i].astype(F32) + update + bias, 0.0).astype(BF16)
             return 0
 
         lax.fori_loop(first + 1, last - 1, conv, 0, unroll=2)
@@ -246,19 +286,57 @@
         lower, part = split(2 * (t - 2) + 1 - LAT_UP + 2 * LAT_UP, LAT_UP)
         return jnp.clip(lower, low_line, high_line), jnp.clip(lower + 1, low_line, high_line), part
 
-    nrows = noise.shape[1]
-    slab = 3 * cin + nrows
+    slab = upper.shape[1]
+    lane = lax.broadcasted_iota(jnp.int32, (1, 128), 1)
+    lane_first, lane_last = lane == 0, lane == 127
+
+    tall = fr + 4
+    for n in range(nout):
+        for j in range(wide):
+            at = slice(j * 128, (j + 1) * 128)
+            base = n * tall
+            grid[j, base + 2:base + 2 + fr, :] = tile[0, n, :, at].astype(F32)
+            above = got_rows[0, :, at].astype(F32)[4 * n + 2:4 * n + 4]
+            below = got_rows[1, :, at].astype(F32)[4 * n:4 * n + 2]
+            grid[j, base:base + 2, :] = jnp.where(top, 0.0, above)
+            grid[j, base + 2 + fr:base + tall, :] = jnp.where(bottom, 0.0, below)
+
+    def along(middle, above, below):
+        above = jnp.where(top, 0.0, pltpu.roll(above.astype(F32), 128 - (fr - 2), 1))
+        below = jnp.where(bottom, 0.0, pltpu.roll(below.astype(F32), fr + 2, 1))
+        middle = pltpu.roll(middle.astype(F32), 2, 1)
+        return jnp.where(lane < 2, above, jnp.where(lane < fr + 2, middle, below))
+
+    west = along(got_cols[0], got_cols[2], got_cols[4])
+    east = along(got_cols[1], got_cols[3], got_cols[5])
+    here = along(own_cols[...], got_cols[6], got_cols[7])
+    none = jnp.zeros((slab - 3 * (cin + nout), 128), F32)
+    left_cols = jnp.concatenate([west[2 * nout:], here[:nout], none], axis=0)
+    right_cols = jnp.concatenate([here[3 * nout:], east[:2 * nout], none], axis=0)
+    west_col, east_col = west[3 * nout:], east[:nout]
+
+    def noise_rows(t):
+        rows = [grid[j, pl.ds(t, nout, stride=tall), :] for j in range(wide)]
+        onward = [pltpu.roll(v, 1, 1) for v in rows]
+        back = [pltpu.roll(v, 127, 1) for v in rows]
+        edge_l = pltpu.roll(west_col, (128 - t) % 128 if isinstance(t, int) else 128 - t, 1)
+        edge_r = pltpu.roll(east_col, 127 - t, 1)
+        pieces = []
+        for j in range(wide):
+            lo = jnp.where(lane_first, onward[j - 1] if j else edge_l, onward[j])
+            hi = jnp.where(lane_last, back[j + 1] if j < wide - 1 else edge_r, back[j])
+            pieces.append(jnp.concatenate([lo, rows[j], hi, none], axis=0))
+        return jnp.concatenate(pieces, axis=1).astype(BF16)
 
     def raise_row(t, slot):
-        a, b, part = lat_split(t)
+        a, b, part = lat_split(jnp.int32(t))
         ok = inside(t)
         wa = jnp.where(ok, 1.0 - part, 0.0)
         wb = jnp.where(ok, part, 0.0)
         for o in range(0, 3 * cin, 16):
             upper[slot, o:o + 16, :] = (wa * lines[a, o:o + 16, :] + wb * lines[b, o:o + 16, :]).astype(BF16)
-        upper[slot, 3 * cin:slab, :] = noise[t]
-
-    lane = lax.broadcasted_iota(jnp.int32, (1, 128), 1)
+        upper[slot, 3 * cin:slab, :] = noise_rows(t)
+
     edge_row = jnp.where(lane < HALF, lane, lane - HALF)
     near = fl // LON_UP
     picked_cols = [-1, 0, near - 1, near]
@@ -291,12 +369,11 @@
             base = p * slab + q * cin
             sides[base:base + cin, :] = jnp.dot(
                 packed, (by_row * by_col).astype(BF16), preferred_element_type=F32).astype(BF16)
-        sides[p * slab + 3 * cin:(p + 1) * slab, :] = noise_edge[p]
+        sides[p * slab + 3 * cin:(p + 1) * slab, :] = jnp.where(
+            lane < HALF, pltpu.roll(left_cols, (128 - p) % 128, 1), pltpu.roll(right_cols, HALF - p, 1)).astype(BF16)
     edge_lift = jnp.dot(liftw[...], sides[...], preferred_element_type=F32) + cols[0]
     edge_lift = edge_lift.astype(BF16).astype(F32)
     edges[...] = jnp.where(inside(edge_row + 1), activate(edge_lift, cols[1]), 0.0)
-
-    lane_first, lane_last = lane == 0, lane == 127
 
     def lift(slot):
         window = jnp.concatenate([upper[(slot + n) % steps] for n in range(3)], axis=0)
@@ -367,10 +444,10 @@
                 rows_out[j, pl.ds(spot + o * group, 16, stride=group), :] = total
 
     for t in range(3):
-        raise_row(jnp.int32(t), t % steps)
+        raise_row(t, t % steps)
     for l in range(3):
         lift(l % steps)
-        raise_row(jnp.int32(l + 3), (l + 3) % steps)
+        raise_row(l + 3, (l + 3) % steps)
         finish(jnp.int32(l), l % steps)
 
     def trip(i, _):
@@ -394,25 +471,26 @@
         pltpu.make_async_copy(stage.at[n % 2], out.at[0, :, pl.ds(n * group, group), :], sems.at[n % 2]).wait()
 
 
-def tile_program(info, got, gain, regw, regb, noise, noise_edge, liftw, liftb, midg, midw, midb, ct):
-    cin, cw = got.shape[1], got.shape[2]
+def tile_program(got, gain, regw, regb, noisy, own_cols, got_cols, got_rows, liftw, liftb, midg, midw, midb, ct):
+    cin, cw = got.shape[2], 2 * got.shape[3]
     ch = liftw.shape[0]
-    fr, fl = noise.shape[0] - 4, noise.shape[2]
-    count = ct + 2
+    nout, fr, fl = noisy.shape[1:]
+    rows = 2 * got.shape[0]
     group = 16
     steps = 4
     vmem = pl.BlockSpec(memory_space=pltpu.VMEM)
-    slab = 3 * cin + noise.shape[1]
+    slab = liftw.shape[1] // 3
     return pl.pallas_call(
         functools.partial(tile_kernel, (cin, ch, ct, fr, fl)),
         out_shape=jax.ShapeDtypeStruct((1, ch, fr, fl), BF16),
-        in_specs=[pl.BlockSpec(memory_space=pltpu.SMEM)] + [vmem] * 11,
+        in_specs=[vmem] * 13,
         out_specs=pl.BlockSpec(memory_space=pl.ANY),
         scratch_shapes=[
-            pltpu.VMEM((got.shape[0] * 3 * cin, cw), BF16),
-            pltpu.VMEM(got.shape, BF16),
+            pltpu.VMEM((fl // 128, nout * (fr + 4), 128), F32),
+            pltpu.VMEM((rows * 3 * cin, cw), BF16),
+            pltpu.VMEM((rows, cin, cw), BF16),
             pltpu.VMEM((cw, 3 * fl), BF16),
-            pltpu.VMEM((count, 3 * cin, fl), F32),
+            pltpu.VMEM((ct + 2, 3 * cin, fl), F32),
             pltpu.VMEM((steps, slab, fl), BF16),
             pltpu.VMEM((3 * slab, 128), BF16),
             pltpu.VMEM((steps, 3 * ch, fl), BF16),
@@ -426,67 +504,37 @@
             pltpu.SemaphoreType.DMA((2,)),
         ],
         compiler_params=pltpu.CompilerParams(vmem_limit_bytes=60_000_000),
-    )(info, got, gain, regw, regb, noise, noise_edge, liftw, liftb, midg, midw, midb)
+    )(got, gain, regw, regb, noisy, own_cols, got_cols, got_rows, liftw, liftb, midg, midw, midb)
 
 
 def per_device(
     coarse, reg_gain, reg_weight, reg_bias, noisy, lift_weight, lift_bias, mid_gain, mid_weight, mid_bias,
 ):
-    device = lax.axis_index("lat")
-    tile_rows = lax.axis_size("lat") // TILE_COLS
     cin, band_rows, clon = coarse.shape
     ct = band_rows * TILE_COLS
     ct_lon = clon // TILE_COLS
     blocks = reg_weight.shape[0]
     ch = lift_weight.shape[2]
-    nout = noisy.shape[1]
-    fr, fl = noisy.shape[2], noisy.shape[3]
-
-    wide = coarse.reshape(cin, band_rows, TILE_COLS, ct_lon)
-    after = jnp.roll(wide, -1, axis=2)
-    before = jnp.roll(wide, 1, axis=2)
-    side = jnp.where(jnp.arange(ct_lon) < ct_lon // 2, after, before)
-    pieces = jnp.concatenate([wide, side], axis=3).transpose(2, 1, 0, 3)
+    nout, fr, fl = noisy.shape[1:]
+
+    quarter = ct_lon // 4
+    centre = coarse.transpose(1, 0, 2).reshape(band_rows, cin, TILE_COLS, ct_lon)
+    after = jnp.roll(centre[..., :quarter], -1, axis=2)
+    before = jnp.roll(centre[..., -quarter:], 1, axis=2)
+    rims = jnp.concatenate([after[0], before[0], after[1], before[1]], axis=-1)
+    pieces = jnp.stack([centre[0], rims, centre[1]]).transpose(2, 0, 1, 3)
 
     tile = noisy[0]
-    edge_cols = jnp.concatenate([tile[:, :, :2], tile[:, :, -2:]], axis=2).transpose(0, 2, 1)
-    edge_cols = jnp.pad(edge_cols.reshape(nout * 4, fr), ((0, 0), (0, 128 - fr)))
-    edge_rows = jnp.concatenate([tile[:, :2], tile[:, -2:]], axis=1).reshape(nout * 4, fl)
-
-    got, got_cols, got_rows = gather(pieces, edge_cols, edge_rows)
-
-    tile_row = device // TILE_COLS
-    has_north = tile_row > 0
-    has_south = tile_row < tile_rows - 1
-    nc = got_cols[:, :, :fr].reshape(6, nout, 4, fr).transpose(0, 1, 3, 2)
-    nr = got_rows.reshape(2, nout, 4, fl)
-    zero = jnp.zeros((), BF16)
-    north = jnp.where(has_north, jnp.concatenate([nc[2][:, -2:, 2:], nr[0][:, 2:], nc[3][:, -2:, :2]], axis=2), zero)
-    south = jnp.where(has_south, jnp.concatenate([nc[4][:, :2, 2:], nr[1][:, :2], nc[5][:, :2, :2]], axis=2), zero)
-    middle = jnp.concatenate([nc[0][:, :, 2:], tile, nc[1][:, :, :2]], axis=2)
-    whole = jnp.concatenate([north, middle, south], axis=1).transpose(1, 0, 2)
-    spare = (-3 * nout) % 16
-    noise = jnp.concatenate(
-        [whole[:, :, 1 + q:1 + q + fl] for q in range(3)] + [jnp.zeros((fr + 4, spare, fl), BF16)], axis=1)
-    sides = []
-    for p in range(3):
-        per_shift = []
-        for q in range(3):
-            lo = jnp.pad(whole[p:p + fr + 2, :, q].T, ((0, 0), (0, HALF - fr - 2)))
-            hi = jnp.pad(whole[p:p + fr + 2, :, fl + 1 + q].T, ((0, 0), (0, HALF - fr - 2)))
-            per_shift.append(jnp.concatenate([lo, hi], axis=1))
-        sides.append(jnp.concatenate(per_shift + [jnp.zeros((spare, 128), BF16)], axis=0))
-    noise_edge = jnp.stack(sides)
-
-    regw = reg_weight.transpose(0, 3, 1, 2, 4).reshape(blocks, cin, 9 * cin)
-    up = lift_weight[..., :cin].transpose(2, 0, 1, 3).reshape(ch, 3, 3 * cin)
-    down = lift_weight[..., cin:].transpose(2, 0, 1, 3).reshape(ch, 3, 3 * nout)
-    liftw = jnp.concatenate([up, down, jnp.zeros((ch, 3, spare), BF16)], axis=2).reshape(ch, -1)
-    midw = mid_weight.transpose(2, 0, 1, 3).reshape(ch, 9 * ch)
-    info = jnp.stack([tile_row, jnp.int32(tile_rows)]).astype(jnp.int32)
-    got = got.reshape((got.shape[0] * band_rows,) + got.shape[2:])
+    edge_cols = jnp.concatenate([tile[:, :, :2], tile[:, :, -2:]], axis=2).transpose(2, 0, 1)
+    edge_cols = jnp.pad(edge_cols.reshape(4 * nout, fr), ((0, 0), (0, 128 - fr)))
+    edge_rows = jnp.concatenate([tile[:, :2], tile[:, -2:]], axis=1).reshape(4 * nout, fl)
+
+    slab = 3 * cin + -(-3 * nout // 16) * 16
+    got, got_cols, got_rows, regw, liftw, midw = gather(
+        pieces, edge_cols, edge_rows, reg_weight.reshape((9 * blocks,) + reg_weight.shape[3:]),
+        lift_weight.reshape((9,) + lift_weight.shape[2:]), mid_weight.reshape((9,) + mid_weight.shape[2:]), slab)
     return tile_program(
-        info, got, reg_gain, regw, reg_bias, noise, noise_edge,
+        got, reg_gain, regw, reg_bias, noisy, edge_cols, got_cols, got_rows,
         liftw, lift_bias[None], mid_gain[None], midw, mid_bias[None], ct)
 
 

time: 73 us -> 64 us (0.88)
  local copies, waits for them, and re-layouts: 13.5 us -> 8.38 us
  other arithmetic: 5.06 us -> 0.9 us
    reshape x9 -> x2, local copies, waits for them, and re-layouts: 4.9 us -> 1.63 us  [the longest x1 1.02 us: per_device(): coarse.transpose(1, 0, 2).reshape(band_rows, cin, TILE_COLS, ct_lon)]
    unnamed x8 -> x4, local copies, waits for them, and re-layouts: 1.09 us -> 3.23 us
    transpose x4 -> x1, local copies, waits for them, and re-layouts: 1.83 us -> 0.01 us  [per_device(): jnp.concatenate([tile[:, :, :2], tile[:, :, -2:]], axis=2)]
    concatenate x4 -> x1, other arithmetic: 1.57 us -> 0.03 us  [per_device(): jnp.concatenate([tile[:, :2], tile[:, -2:]], axis=1).reshape(4 * nout, fl)]
    another operation x3 -> x1, other arithmetic: 1.36 us -> 0.14 us  [per_device(): pieces = jnp.stack([centre[0], rims, centre[1]]).transpose(2, 0, 1, 3)]
    transpose x2, other arithmetic: 1.93 us -> 0.74 us  [the longest x1 0.73 us: per_device(): pieces = jnp.stack([centre[0], rims, centre[1]]).transpose(2, 0, 1, 3)]
    slice x24 -> x7, local copies, waits for them, and re-layouts: 2.98 us -> 2.18 us  [the longest x5 1.79 us: per_device(): pieces = jnp.stack([centre[0], rims, centre[1]]).transpose(2, 0, 1, 3)]
    select_n x2 -> x0, local copies, waits for them, and re-layouts: 0.78 us -> none  [the longest x1 0.39 us: per_device(): jnp.where(has_north, jnp.concatenate([nc[2][:, -2:, 2:], nr[0][:, 2:], nc...]
where the time goes in v3:
time: 64 us; the launch traced here: 63.7 us
  Pallas kernels  54.3 us (85%)
  local copies, waits for them, and re-layouts  8.38 us (13%)
  other arithmetic  0.9 us (1%)
    pallas_call x1, Pallas kernels, tile_program(): pl.pallas_call(functools.partial(tile_kernel, (cin, ch, ct, fr, fl)), out...  39.7 us
    pallas_call x1, Pallas kernels, gather(): pl.pallas_call(gather_kernel, out_shape=(jax.ShapeDtypeStruct((8,) + piec...  14.6 us
    unnamed x4, local copies, waits for them, and re-layouts  3.23 us
    slice x5, local copies, waits for them, and re-layouts, per_device(): pieces = jnp.stack([centre[0], rims, centre[1]]).transpose(2, 0, 1, 3)  1.79 us

profile of v3, /device:TPU:0, one launch (start us, length us, event | category | flops | bytes accessed | tf_op | source)
XLA Modules:
  0.0 63.7 jit_solution(7001996936896282907)
XLA Ops:
  0.0 1.0 %reshape.26 = bf16[2,80,4,128]{3,2,0,1:T(4,128)(2,1)S(1)} reshape(bf16[2,80,512]{2,0,1:T(2,128)(2,1)} %bitcast.28) | data formatting | bytes 327680 | tf_op jit(solution)/shard_map/reshape | solution.py:521
  1.0 0.2 fusion.2
  1.2 0.2 fusion.3
  1.6 0.1 maximum_bitcast_fusion.1
  1.7 1.7 %slice_reduce_fusion.1 = (bf16[80,512]{1,0:T(8,128)(2,1)S(1)}, bf16[80,512]{1,0:T(8,128)(2,1)S(1)}) fusion(bf16[2,80,512]{2,0,1:T(2,128)(2,1)} %bitcast.29), kind=kLoop, calls=%fused_computation.2 | loop fusion | bytes 327680 | tf_op jit(solution)/shard_map/slice | solution.py:525
  3.5 0.7 %maximum_bitcast_fusion.pieces = bf16[4,3,80,128]{3,2,1,0:T(8,128)(2,1)} fusion(bf16[1,80,4,128]{3,1,0,2:T(8,128)(2,1)S(1)} %copy.59, bf16[1,80,4,128]{3,1,0,2:T(8,128)(2,1)S(1)} %maximum_bitcast_fusion.1, bf16[1,80,4,128]{3,1,0,2:T(8,128)(2,1)S(1)} %copy.58), kind=kLoop, calls=%fused_computation | loop fusion | flops 245760 | bytes 491520 | tf_op jit(solution)/shard_map/transpose | solution.py:525
  4.3 2.0 %copy.64 = bf16[3,3,192,84]{3,2,1,0:T(8,128)(2,1)} copy(bf16[3,3,192,84]{2,3,1,0:T(8,128)(2,1)} %param.15) | data formatting | bytes 580608 | tf_op args[5]
  6.3 1.2 %copy.60 = bf16[1,4,32,512]{2,3,1,0:T(8,128)(2,1)S(1)} copy(bf16[1,4,32,512]{3,2,1,0:T(8,128)(2,1)} %tile.1) | data formatting | bytes 262144 | tf_op args[4]
  7.5 0.6 pad.4.cols.own_cols
  8.1 0.2 fusion
  8.3 0.2 copy.62
  8.5 0.2 copy.63
  8.8 0.6 reshape.22.rows
  9.4 14.6 %shard_map.100 = (bf16[8,3,80,128]{3,2,1,0:T(8,128)(2,1)}, bf16[8,16,128]{2,1,0:T(8,128)(2,1)}, bf16[2,16,512]{2,1,0:T(8,128)(2,1)}, bf16[2,80,720]{2,1,0:T(8,12...) custom-call(bf16[4,3,80,128]{3,2,1,0:T(8,128)(2,1)} %maximum_bitcast_fusion.pieces, ...), custom_call_target="tpu_custom_call" | custom-call | tf_op jit(solution)/shard_map/pallas_call | solution.py:157
  24.0 39.7 %shard_map.101 = bf16[1,192,32,512]{3,2,1,0:T(8,128)(2,1)} custom-call(bf16[8,3,80,128]{3,2,1,0:T(8,128)(2,1)} %get-tuple-element.11.got, f32[2,80]{1,0:T(2,128)} %gain.1, bf16[2,80,720]{2,1,0:T(8,128)(2,1)} %get-tuple-element.12.regw, f32[2,80]{1,0:T(2,128)} %regb.1, bf16[1,4,32,512]{3,2,1,0:T(8,128)(2,1)} %tile.1, bf16[16,128]{1,0:T(8,128)(2,1)} %pad.4.cols.own_cols, ...), custom_call_target="tpu_custom_call" | custom-call | tf_op jit(solution)/shard_map/pallas_call | solution.py:483
  (13 shorter events, 0.2 us)

commit v4 on v3

--- a/solution.py
+++ b/solution.py
@@ -53,7 +53,7 @@
             src_ref=src, dst_ref=dst, send_sem=ssem, recv_sem=rsem,
             device_id={"lat": target}, device_id_type=MESH)
 
-    whole, upper, lower = pl.ds(0, 3), pl.ds(0, 2), pl.ds(1, 2)
+    whole, upper, lower = pl.ds(0, 2), pl.ds(0, 1), pl.ds(1, 1)
 
     def band_copy(k, row, slot, ssem, part=whole):
         col = (c + k) % TILE_COLS
@@ -223,14 +223,9 @@
             taps[pl.ds(base + 2 * cin, cin), :] = pltpu.roll(values, cw - 1, 1).astype(BF16)
 
         def fill_first(n, _, fill=fill):
-            rims = got[n, 1].astype(F32)
-            turned = pltpu.roll(rims, cw // 4, 1)
             for sub in range(2):
-                rim = jnp.where(lax.broadcasted_iota(jnp.int32, (1, cw // 2), 1) < cw // 8,
-                                turned if sub else rims, rims if sub else turned)
-                values = jnp.concatenate([got[n, 2 * sub].astype(F32), rim], axis=1)
-                field[2 * n + sub] = values.astype(BF16)
-                fill(2 * n + sub, values)
+                field[2 * n + sub] = got[n, sub]
+                fill(2 * n + sub, got[n, sub].astype(F32))
             return 0
 
         def fill_next(i, _, fill=fill):
@@ -472,7 +467,7 @@
 
 
 def tile_program(got, gain, regw, regb, noisy, own_cols, got_cols, got_rows, liftw, liftb, midg, midw, midb, ct):
-    cin, cw = got.shape[2], 2 * got.shape[3]
+    cin, cw = got.shape[2:]
     ch = liftw.shape[0]
     nout, fr, fl = noisy.shape[1:]
     rows = 2 * got.shape[0]
@@ -517,12 +512,11 @@
     ch = lift_weight.shape[2]
     nout, fr, fl = noisy.shape[1:]
 
-    quarter = ct_lon // 4
-    centre = coarse.transpose(1, 0, 2).reshape(band_rows, cin, TILE_COLS, ct_lon)
-    after = jnp.roll(centre[..., :quarter], -1, axis=2)
-    before = jnp.roll(centre[..., -quarter:], 1, axis=2)
-    rims = jnp.concatenate([after[0], before[0], after[1], before[1]], axis=-1)
-    pieces = jnp.stack([centre[0], rims, centre[1]]).transpose(2, 0, 1, 3)
+    blocked = coarse.reshape(cin, band_rows, TILE_COLS, ct_lon)
+    after = jnp.roll(blocked, -1, axis=2)
+    before = jnp.roll(blocked, 1, axis=2)
+    side = jnp.where(jnp.arange(ct_lon) < ct_lon // 2, after, before)
+    pieces = jnp.concatenate([blocked, side], axis=3).transpose(2, 1, 0, 3)
 
     tile = noisy[0]
     edge_cols = jnp.concatenate([tile[:, :, :2], tile[:, :, -2:]], axis=2).transpose(2, 0, 1)

time: 64 us -> 62 us (0.969)
  local copies, waits for them, and re-layouts: 8.38 us -> 6.15 us
    slice x7 -> x2, local copies, waits for them, and re-layouts: 2.18 us -> 0.04 us  [per_device(): before = jnp.roll(blocked, 1, axis=2)]
    pallas_call x1, Pallas kernels: 14.6 us -> 15.4 us  [gather(): pl.pallas_call(gather_kernel, out_shape=(jax.ShapeDtypeStruct((8,) + piec...]
    unnamed x4 -> x2, local copies, waits for them, and re-layouts: 3.23 us -> 3.19 us
where the time goes in v4:
time: 62 us; the launch traced here: 61.8 us
  Pallas kernels  54.7 us (88%)
  local copies, waits for them, and re-layouts  6.15 us (10%)
  other arithmetic  0.85 us (1%)
    pallas_call x1, Pallas kernels, tile_program(): pl.pallas_call(functools.partial(tile_kernel, (cin, ch, ct, fr, fl)), out...  39.3 us
    pallas_call x1, Pallas kernels, gather(): pl.pallas_call(gather_kernel, out_shape=(jax.ShapeDtypeStruct((8,) + piec...  15.4 us
    unnamed x2, local copies, waits for them, and re-layouts  3.19 us

profile of v4, /device:TPU:0, one launch (start us, length us, event | category | flops | bytes accessed | tf_op | source)
XLA Modules:
  0.0 61.8 jit_solution(13883521284547204189)
XLA Ops:
  0.0 1.0 %reshape.24 = bf16[80,2,4,128]{3,2,1,0:T(4,128)(2,1)S(1)} reshape(bf16[80,2,512]{2,1,0:T(2,128)(2,1)} %param.10) | data formatting | bytes 327680 | tf_op jit(solution)/shard_map/reshape | solution.py:515
  1.2 0.8 %maximum_bitcast_fusion.pieces = bf16[4,2,80,256]{3,2,1,0:T(8,128)(2,1)} fusion(bf16[80,2,4,128]{3,0,1,2:T(8,128)(2,1)S(1)} %maximum_select_fusion, bf16[80,2,4,128]{3,0,1,2:T(8,128)(2,1)S(1)} %copy.36), kind=kLoop, calls=%fused_computation | loop fusion | flops 655360 | bytes 655360 | tf_op jit(solution)/shard_map/transpose | solution.py:519
  1.9 2.0 %copy.41 = bf16[3,3,192,84]{3,2,1,0:T(8,128)(2,1)} copy(bf16[3,3,192,84]{2,3,1,0:T(8,128)(2,1)} %param.15) | data formatting | bytes 580608 | tf_op args[5]
  3.9 1.2 %copy.37 = bf16[1,4,32,512]{2,3,1,0:T(8,128)(2,1)S(1)} copy(bf16[1,4,32,512]{3,2,1,0:T(8,128)(2,1)} %tile.1) | data formatting | bytes 262144 | tf_op args[4]
  5.2 0.6 pad.4.cols.own_cols
  5.8 0.2 fusion
  6.0 0.2 copy.39
  6.2 0.2 copy.40
  6.5 0.6 reshape.20.rows
  7.1 15.4 %shard_map.100 = (bf16[8,2,80,256]{3,2,1,0:T(8,128)(2,1)}, bf16[8,16,128]{2,1,0:T(8,128)(2,1)}, bf16[2,16,512]{2,1,0:T(8,128)(2,1)}, bf16[2,80,720]{2,1,0:T(8,12...) custom-call(bf16[4,2,80,256]{3,2,1,0:T(8,128)(2,1)} %maximum_bitcast_fusion.pieces, ...), custom_call_target="tpu_custom_call" | custom-call | tf_op jit(solution)/shard_map/pallas_call | solution.py:157
  22.5 39.3 %shard_map.101 = bf16[1,192,32,512]{3,2,1,0:T(8,128)(2,1)} custom-call(bf16[8,2,80,256]{3,2,1,0:T(8,128)(2,1)} %get-tuple-element.11.got, f32[2,80]{1,0:T(2,128)} %gain.1, bf16[2,80,720]{2,1,0:T(8,128)(2,1)} %get-tuple-element.12.regw, f32[2,80]{1,0:T(2,128)} %regb.1, bf16[1,4,32,512]{3,2,1,0:T(8,128)(2,1)} %tile.1, bf16[16,128]{1,0:T(8,128)(2,1)} %pad.4.cols.own_cols, ...), custom_call_target="tpu_custom_call" | custom-call | tf_op jit(solution)/shard_map/pallas_call | solution.py:478
  (9 shorter events, 0.2 us)
